TPU v7x, 32 devices: a whole 2x2x4 slice. The times are simulated.
32 devices in a mesh: doc: 4 (over y, x), seq: 8 (over z, core).
Axes of the slice: x: 2, y: 2, z: 4, core: 2. Of those that a mesh axis runs over, the one named last changes fastest.
Arguments:
- queries: bfloat16 [12288, 2048], P(('doc', 'seq')), parts along dimension 0, may hold values from -120 to 120
- keys: bfloat16 [12288, 2048], P(('doc', 'seq')), parts along dimension 0, may hold values from -4.1 to 4.1
- values: bfloat16 [12288, 2048], P(('doc', 'seq')), parts along dimension 0, may hold values from -6 to 6
- global_positions: int32 [256], P('doc'), parts along dimension 0, may hold values from 0 to 3070, as said below
- score_weight: float32 [2048], replicated, may hold values from -0.125 to 0.125
Outputs:
- token_scores: float32 [12288], P(('doc', 'seq')), parts along dimension 0
There are 4 independent parts, one for each index of `doc`. A program takes and returns all parts, laid end to end along the dimension named above; an argument that names none is the same for every part. Nothing has to cross between parts.
Inputs may be any that keep to these rules, and one draw needn't show every extreme that they name: `global_positions`: 64 distinct positions in increasing order; the first is 0 and the last is 3070.
All inputs are finite; a program needn't handle non-finite values.
Results may differ from a plain program's by a relative error of at most 0.0023.
Values may be sent and summed in bfloat16 or wider, within the bound.
No kernel may reach another device: no remote copies, remote signals or barrier semaphores. Data moves between devices by JAX's collectives and lax.ppermute only.
A program may use at most 64 MiB of HBM per device.

v0:
```python
import jax
import jax.numpy as jnp
from jax import lax
from jax.sharding import PartitionSpec as P

HEADS = 16
BLK = 64


def extended(block, sides, width):
    for axis, dim in sides:
        count = lax.axis_size(axis)
        forward = [(i, i + 1) for i in range(count - 1)]
        backward = [(target, source) for source, target in forward]
        low = lax.ppermute(
            lax.slice_in_dim(block, block.shape[dim] - width, None, axis=dim), axis, forward
        )
        high = lax.ppermute(lax.slice_in_dim(block, 0, width, axis=dim), axis, backward)
        block = jnp.concatenate([low, block, high], axis=dim)
    return block


def token_score(attended, score_weight):
    mean_square = jnp.mean(attended * attended, axis=-1)
    return jnp.sum(attended * score_weight, axis=-1) * lax.rsqrt(mean_square + 1e-06)


def on_device(queries, keys, values, global_positions, score_weight):
    row_count, model_width = queries.shape
    head_count = HEADS
    head_size = model_width // head_count
    block_rows = BLK
    local_blocks = row_count // block_rows
    glob_count = global_positions.shape[0]
    seq_index = lax.axis_index("seq")
    seq_count = lax.axis_size("seq")
    block_total = local_blocks * seq_count
    score_scale = head_size ** (-0.5)
    row_ids = seq_index * row_count + jnp.arange(row_count, dtype=jnp.int32)
    selected = global_positions[:, None] == row_ids[None, :]
    select_mat = selected.astype(jnp.bfloat16)
    glob_parts = (
        jnp.dot(select_mat, queries, preferred_element_type=jnp.float32).astype(jnp.bfloat16),
        jnp.dot(select_mat, keys, preferred_element_type=jnp.float32).astype(jnp.bfloat16),
        jnp.dot(select_mat, values, preferred_element_type=jnp.float32).astype(jnp.bfloat16),
    )
    glob_q, glob_k, glob_v = (
        lax.psum(glob_parts[0], "seq").astype(jnp.float32),
        lax.psum(glob_parts[1], "seq").astype(jnp.float32),
        lax.psum(glob_parts[2], "seq").astype(jnp.float32),
    )
    glob_q = glob_q.astype(jnp.bfloat16).reshape(glob_count, head_count, head_size)
    glob_k = glob_k.astype(jnp.bfloat16).reshape(glob_count, head_count, head_size)
    glob_v = glob_v.astype(jnp.bfloat16).reshape(glob_count, head_count, head_size)
    glob_block = global_positions // block_rows
    joined = jnp.concatenate((keys, values), axis=1)
    padded = extended(joined, (("seq", 0),), block_rows)
    padded = padded.reshape(local_blocks + 2, block_rows, 2, head_count, head_size)
    key_pad = padded[:, :, 0]
    value_pad = padded[:, :, 1]
    query_blocks = queries.reshape(local_blocks, block_rows, head_count, head_size)
    block_ids = seq_index * local_blocks + jnp.arange(local_blocks, dtype=jnp.int32)
    score_list = []
    valid_list = []
    for offset in range(3):
        score_list.append(
            jnp.einsum(
                "nqhd,nkhd->nhqk",
                query_blocks,
                key_pad[offset : offset + local_blocks],
                preferred_element_type=jnp.float32,
            )
        )
        key_block = block_ids + (offset - 1)
        in_range = (key_block >= 0) & (key_block < block_total)
        valid_list.append(jnp.broadcast_to(in_range[:, None], (local_blocks, block_rows)))
    score_list.append(
        jnp.einsum("nqhd,ghd->nhqg", query_blocks, glob_k, preferred_element_type=jnp.float32)
    )
    valid_list.append(jnp.abs(glob_block[None, :] - block_ids[:, None]) > 1)
    scores = jnp.concatenate(score_list, axis=-1) * score_scale
    key_valid = jnp.concatenate(valid_list, axis=-1)[:, None, None, :]
    scores = jnp.where(key_valid, scores, -jnp.inf)
    row_max = jnp.max(scores, axis=-1, keepdims=True)
    exp_scores = jnp.exp(scores - row_max)
    row_total = jnp.sum(exp_scores, axis=-1)
    weights = exp_scores.astype(jnp.bfloat16)
    mixture = jnp.einsum(
        "nhqg,ghd->nqhd", weights[..., 3 * block_rows :], glob_v, preferred_element_type=jnp.float32
    )
    for offset in range(3):
        mixture = mixture + jnp.einsum(
            "nhqk,nkhd->nqhd",
            weights[..., offset * block_rows : (offset + 1) * block_rows],
            value_pad[offset : offset + local_blocks],
            preferred_element_type=jnp.float32,
        )
    window_out = (mixture / jnp.transpose(row_total, (0, 2, 1))[..., None]).reshape(
        row_count, model_width
    )
    window_score = token_score(window_out, score_weight)
    local_keys = keys.reshape(row_count, head_count, head_size)
    local_values = values.reshape(row_count, head_count, head_size)
    glob_scores = (
        jnp.einsum("ghd,khd->hgk", glob_q, local_keys, preferred_element_type=jnp.float32)
        * score_scale
    )
    seg_max = jnp.max(glob_scores, axis=-1)
    glob_exp = jnp.exp(glob_scores - seg_max[..., None])
    seg_total = jnp.transpose(jnp.sum(glob_exp, axis=-1))
    seg_peak = jnp.transpose(seg_max)
    seg_acc = jnp.einsum(
        "hgk,khd->ghd",
        glob_exp.astype(jnp.bfloat16),
        local_values,
        preferred_element_type=jnp.float32,
    )
    top_peak = lax.pmax(seg_peak, "seq")
    rescale = jnp.exp(seg_peak - top_peak)
    scaled_acc = (seg_acc * rescale[..., None]).reshape(glob_count, model_width)
    acc_whole, total_whole = lax.psum((scaled_acc, seg_total * rescale), "seq")
    glob_out = (
        acc_whole.reshape(glob_count, head_count, head_size) / total_whole[:, :, None]
    ).reshape(glob_count, model_width)
    glob_score = token_score(glob_out, score_weight)
    placement = jnp.transpose(selected).astype(jnp.float32)
    is_global = jnp.any(selected, axis=0)
    placed = jnp.dot(placement, glob_score, precision=lax.Precision.HIGHEST)
    return jnp.where(is_global, placed, window_score)


def solution(mesh):
    placed = (
        P(("doc", "seq"), None),
        P(("doc", "seq"), None),
        P(("doc", "seq"), None),
        P("doc"),
        P(),
    )
    return jax.shard_map(
        on_device, mesh=mesh, in_specs=placed, out_specs=P(("doc", "seq")), check_vma=False
    )
```

profile of v0, /device:TPU:0, one launch (start us, length us, event | category | flops | bytes accessed | tf_op | source)
XLA Modules:
  0.0 179.3 jit_solution(5734152668019470307)
XLA Ops:
  6.5 1.6 constant_dynamic-update-slice_fusion.1
  8.2 0.2 copy-done
  8.4 0.2 constant_dynamic-update-slice_fusion
  8.6 1.7 copy-done.3
  10.3 1.1 fusion.67
  11.3 3.2 %collective-permute-start = (bf16[64,4096]{1,0:T(8,128)(2,1)}, bf16[64,4096]{1,0:T(8,128)(2,1)}, u32[]{:S(2)}, u32[]{:S(2)}) collective-permute-start(bf16[64,4096]{1,0:T(8,128)(2,1)} %get-tuple-element.26), channel_id=1, source_target_pairs={{0,1},{1,2},{2,3},{3,4},{4,5},{5,6},{6,7},{8,9},{9,10},{10,11},{11... | collective-permute-start | bytes 1572872 | tf_op jit(solution)/shard_map/ppermute | solution.py:15
  14.5 1.3 collective-permute-start.1
  15.8 0.4 fusion.32
  16.3 0.4 fusion.31
  16.7 0.8 copy.163
  17.5 0.2 copy-done.5
  17.7 0.4 fusion.30
  18.1 0.9 copy_bitcast_fusion.13
  19.1 0.1 abs_compare_fusion
  19.2 1.8 %copy.102 = bf16[48,8,16,128]{3,2,1,0:T(8,128)(2,1)S(1)} copy(bf16[48,8,16,128]{3,1,2,0:T(8,128)(2,1)} %bitcast.131) | data formatting | bytes 3145728
  21.0 0.1 broadcast_in_dim.14
  21.1 0.1 broadcast_in_dim.16
  21.3 0.1 pad_add_fusion
  21.3 0.1 compare_reduce_fusion
  21.4 59.4 %all-reduce.6.cloned.1.call-done = (bf16[64,16,128]{2,0,1:T(8,128)(2,1)}, bf16[64,16,128]{2,0,1:T(8,128)(2,1)}, bf16[64,16,128]{2,0,1:T(8,128)(2,1)}) async-done(((bf16[64,16,128]{2,0,1:T(8,128)(2,1)}, bf16[64,16,128]{2,0,1:T(8,128)(2,1)}, bf16[64,16,128]{2,0,1:T(8,128)(2,1)}), (bf16[64,16,128]{2,0,1:T(8,128)(2,1)}, bf16[64,16,128]{2,0,1:T(8,128)(2,1)}, ...) | async-done | bytes 786448 | tf_op jit(solution)/shard_map/psum | solution.py:48
  80.8 3.5 %fusion.68 = (f32[16,64]{1,0:T(8,128)S(1)}, f32[16,64,384]{2,1,0:T(8,128)}) fusion(bf16[64,16,128]{2,0,1:T(8,128)(2,1)} %get-tuple-element.9, bf16[384,2048]{1,0:T(8,128)(2,1)} %param.6), kind=kOutput, calls=%fused_computation.105 | convolution fusion | flops 101448704 | bytes 3411968 | tf_op jit(solution)/shard_map/ghd,khd->hgk/dot_general | solution.py:105
  84.3 13.9 %pmax.7 = f32[64,16]{0,1:T(8,128)S(1)} all-reduce(f32[64,16]{0,1:T(8,128)S(1)} %bitcast.135), channel_id=1, replica_groups=mesh['doc'=4,'seq'=8] {'seq'}, use_global_device_ids=true, to_apply=%region_3.4 | all-reduce | flops 1024 | bytes 8192 | tf_op jit(solution)/shard_map/pmax | solution.py:118
  98.2 2.0 %fusion.19 = f32[16,64]{1,0:T(8,128)S(1)} fusion(f32[16,64,384]{2,1,0:T(8,128)} %get-tuple-element.29, f32[16,64]{1,0:T(8,128)S(1)} %get-tuple-element.28), kind=kLoop, calls=%fused_computation.39 | loop fusion | flops 785408 | bytes 1581056 | tf_op jit(solution)/shard_map/reduce_sum | solution.py:110
  100.2 0.8 fusion.27
  101.0 0.8 copy.162
  101.9 14.0 %psum.37 = f32[64,16]{0,1:T(8,128)S(1)} all-reduce(f32[64,16]{0,1:T(8,128)S(1)} %get-tuple-element.12), channel_id=1, replica_groups=mesh['doc'=4,'seq'=8] {'seq'}, use_global_device_ids=true, to_apply=%region_6.7 | all-reduce | flops 1024 | bytes 8192 | tf_op jit(solution)/shard_map/psum | solution.py:121
  116.0 0.1 copy.69
  116.1 0.6 convolution_bitcast_fusion
  116.6 1.3 copy-done.4
  118.0 1.4 maximum_bitcast_fusion
  119.3 1.2 copy.101
  120.6 2.1 %fusion.65 = (bf16[6,64,1,16,128]{4,3,2,1,0:T(8,128)(2,1)S(1)}, bf16[6,64,1,16,128]{4,3,2,1,0:T(8,128)(2,1)S(1)}, bf16[6,64,1,16,128]{4,3,2,1,0:T(8,128)(2,1)S(1...) fusion(bf16[8,64,2,16,128]{4,3,2,1,0:T(8,128)(2,1)S(1)} %bitcas, ...), kind=kLoop, calls=%fused_computation.102 | loop fusion | bytes 18874368 | tf_op jit(solution)/shard_map/slice | solution.py:95
  122.7 1.0 convolution_bitcast_fusion.1
  123.7 1.0 convolution_bitcast_fusion.2
  124.6 2.6 %convolution_bitcast_fusion.3 = f32[6,16,64,64]{3,2,1,0:T(8,128)} fusion(bf16[6,64,1,16,128]{4,3,2,1,0:T(8,128)(2,1)S(1)} %get-tuple-element.20, bf16[6,64,16,128]{3,2,1,0:T(8,128)(2,1)S(1)} %bitcast.130), kind=kOutput, calls=%fused_computation.17 | convolution fusion | flops 100663296 | bytes 4718592 | tf_op jit(solution)/shard_map/nqhd,nkhd->nhqk/dot_general | solution.py:67
  127.3 36.3 %fusion.64 = (f32[6,16,64]{2,1,0:T(8,128)S(1)}, bf16[6,16,64,256]{3,2,1,0:T(8,128)(2,1)S(1)}) fusion(f32[6,16,64,64]{3,2,1,0:T(8,128)S(1)} %convolution_bitcast_fusion, f32[6,16,64,64]{3,2,1,0:T(8,128)S(1)} %convolution_bitcast_fusion.1, f32[6,16,64,64]{3,2,1,0:T(8,128)S(1)} %convolution_bitcast_fusion.2, f32[6,16,64,64]{3,2,1,0:T(8,128)} %convolution_bitcast_fusion.3, ...), kind=kOutput, calls=%fused_computation.101 | output fusion | flops 12583167 | bytes 9463296 | tf_op jit(solution)/shard_map/sub | solution.py:85
  163.6 1.8 %fusion.66 = (bf16[6,16,64,64]{3,2,1,0:T(8,128)(2,1)S(1)}, bf16[6,16,64,64]{3,2,1,0:T(8,128)(2,1)S(1)}, bf16[6,16,64,64]{3,2,1,0:T(8,128)(2,1)S(1)}, bf16[6,16,64,64]{3,2,1,0:T(8,128)(2,1)S(1)}) fusion(bf16[6,16,64,256]{3,2,1,0:T(8,128)(2,1)S(1)} %get-tuple-element.15), kind=kLoop, calls=%fused_computation.103 | loop fusion | bytes 6291456 | tf_op jit(solution)/shard_map/slice | solution.py:94
  165.4 0.7 fusion.9
  166.1 0.7 fusion.10
  166.9 0.2 copy-done.6
  167.1 0.5 fusion.14
  167.6 0.1 copy-done.8
  167.8 2.1 %multiply_reduce_fusion = (f32[6,64]{1,0:T(8,128)S(1)}, f32[6,64]{1,0:T(8,128)S(1)}) fusion(f32[16,128]{1,0:T(8,128)S(1)} %bitcast.137, f32[6,64,16]{1,0,2:T(8,128)S(1)} %copy.86, bf16[6,64,1,16,128]{4,3,2,1,0:T(8,128)(2,1)S(1)} %get-tuple-element.16, bf16[6,16,64,64]{3,2,1,0:T(8,128)(2,1)S(1)} %get-tuple-element.22, f32[6,16,128,64]{2,3,0,1:T(8,128)S(1)} %fusion.9, ...), kind=kOutput, calls=%fused_computation.9 | convolution fusion | flops 106953984 | bytes 11832320 | tf_op jit(solution)/shard_map/nhqk,nkhd->nqhd/dot_general | solution.py:92
  169.9 0.1 mul.82
  170.0 0.2 div.43
  170.2 1.3 multiply_reduce_fusion.2
  171.5 0.3 convolution_reduce_fusion
  171.9 0.6 select_n.15
  (30 shorter events, 0.3 us)
Async XLA Ops:
  6.5 1.9 %copy-start = (bf16[384,2048]{1,0:T(8,128)(2,1)S(1)}, bf16[384,2048]{1,0:T(8,128)(2,1)}, u32[]{:S(2)}) copy-start(bf16[384,2048]{1,0:T(8,128)(2,1)} %param.7) | copy-start | bytes 4718596
  6.5 74.3 %all-reduce.6.cloned.1.call-start = ((), (), s32[]{:S(2)}) async-start(), calls=%async_computation.1 | async-start | bytes 1572864 | tf_op jit(solution)/shard_map/psum | solution.py:48
  8.6 1.7 copy-start.3
  10.3 5.5 %copy-start.1 = (bf16[384,2048]{1,0:T(8,128)(2,1)S(1)}, bf16[384,2048]{1,0:T(8,128)(2,1)}, u32[]{:S(2)}) copy-start(bf16[384,2048]{1,0:T(8,128)(2,1)} %param.6) | copy-start | bytes 4718596
  10.3 5.5 %copy-start.9 = (s32[64]{0:T(128)S(1)}, s32[64]{0:T(128)}, u32[]{:S(2)}) copy-start(s32[64]{0:T(128)} %param.8) | copy-start | bytes 772
  11.3 105.3 %collective-permute-start = (bf16[64,4096]{1,0:T(8,128)(2,1)}, bf16[64,4096]{1,0:T(8,128)(2,1)}, u32[]{:S(2)}, u32[]{:S(2)}) collective-permute-start(bf16[64,4096]{1,0:T(8,128)(2,1)} %get-tuple-element.26), channel_id=1, source_target_pairs={{0,1},{1,2},{2,3},{3,4},{4,5},{5,6},{6,7},{8,9},{9,10},{10,11},{11... | collective-permute-start | bytes 1572872 | tf_op jit(solution)/shard_map/ppermute | solution.py:15
  14.5 102.2 %collective-permute-start.1 = (bf16[64,4096]{1,0:T(8,128)(2,1)}, bf16[64,4096]{1,0:T(8,128)(2,1)}, u32[]{:S(2)}, u32[]{:S(2)}) collective-permute-start(bf16[64,4096]{1,0:T(8,128)(2,1)} %get-tuple-element.27), channel_id=1, source_target_pairs={{1,0},{2,1},{3,2},{4,3},{5,4},{6,5},{7,6},{9,8},{10,9},{11,10},{12... | collective-permute-start | bytes 1572872 | tf_op jit(solution)/shard_map/ppermute | solution.py:18
  16.2 1.4 copy-start.5
  19.1 150.9 %all-reduce.4.cloned.1.call-start = ((), (), s32[]{:S(2)}) async-start(), calls=%async_computation | async-start | bytes 1048576 | tf_op jit(solution)/shard_map/psum | solution.py:121
  98.2 2.0 %copy-start.2 = (f32[16,64,384]{2,1,0:T(8,128)S(1)}, f32[16,64,384]{2,1,0:T(8,128)}, u32[]{:S(2)}) copy-start(f32[16,64,384]{2,1,0:T(8,128)} %get-tuple-element.29) | copy-start | bytes 4718596
  101.0 15.0 %copy-start.7 = (bf16[64,16,128]{2,0,1:T(8,128)(2,1)S(1)}, bf16[64,16,128]{2,0,1:T(8,128)(2,1)}, u32[]{:S(2)}) copy-start(bf16[64,16,128]{2,0,1:T(8,128)(2,1)} %get-tuple-element.10) | copy-start | bytes 786436
  116.0 1.9 %copy-start.4 = (bf16[384,4096]{1,0:T(8,128)(2,1)S(1)}, bf16[384,4096]{1,0:T(8,128)(2,1)}, u32[]{:S(2)}) copy-start(bf16[384,4096]{1,0:T(8,128)(2,1)} %copy-done.3) | copy-start | bytes 9437188
  166.1 1.0 copy-start.6
  167.1 0.7 copy-start.8
Sparse Core Ops, SparseCore 0:
  19.2 61.5 all-reduce.5
  102.0 54.4 all-reduce.3
where the time goes:
time: 180 us; the launch traced here: 179 us
  waiting for transfers between devices  59.4 us (33%)
  other arithmetic  41.9 us (23%)
  blocking collectives  28 us (16%)
  local copies, waits for them, and re-layouts  16.8 us (9%)
  matrix products  15.1 us (8%)
  between operations  13.7 us (8%)
  starting transfers between devices  4.48 us (2%)
    psum x1, waiting for transfers between devices, on_device(): lax.psum(glob_parts[0], 'seq').astype(jnp.float32)  59.4 us
    sub x1, other arithmetic, on_device(): exp_scores = jnp.exp(scores - row_max)  36.3 us
    psum x1, blocking collectives, on_device(): acc_whole, total_whole = lax.psum((scaled_acc, seg_total * rescale), 'seq')  14 us
    pmax x1, blocking collectives, on_device(): top_peak = lax.pmax(seg_peak, 'seq')  13.9 us
    unnamed x23, local copies, waits for them, and re-layouts  8.46 us
    dot_general x3, matrix products, on_device(): jnp.einsum('nqhd,nkhd->nhqk', query_blocks, key_pad[offset:offset + local...  4.54 us
  transfers between devices with their start and end apart: 4, of which 1 were waited for; matrix products, arithmetic and copies ran while one was open for 36% of the time, Pallas kernels for 0%

commit v1 on v0

v1 whole, which is shorter than its diff:
```python
import functools
import math

import jax
import jax.numpy as jnp
from jax import lax
from jax.experimental import pallas as pl
from jax.experimental.pallas import tpu as pltpu
from jax.sharding import PartitionSpec as P

HEADS = 16
BLK = 64
CORES = 2
LANES = 128
NEG = -1e30
LOG2E = math.log2(math.e)
STAT_ROWS = 16


def pieces(x):
    hi = x.astype(jnp.bfloat16)
    rest = x - hi.astype(jnp.float32)
    mid = rest.astype(jnp.bfloat16)
    low = (rest - mid.astype(jnp.float32)).astype(jnp.bfloat16)
    return hi, mid, low


def dot_t(a, b):
    return lax.dot_general(a, b, (((1,), (1,)), ((), ())), preferred_element_type=jnp.float32)


def dot_n(a, b):
    return lax.dot_general(a, b, (((1,), (0,)), ((), ())), preferred_element_type=jnp.float32)


def put_message(out_ref, pair, out, peak, total):
    rows = out.shape[0]
    out_ref[pair, :rows, :] = out.astype(jnp.bfloat16)
    stats = [p.astype(jnp.float32) for p in (*pieces(peak), *pieces(total))]
    row = lax.broadcasted_iota(jnp.int32, (STAT_ROWS, LANES), 0)
    block = jnp.zeros((STAT_ROWS, LANES), jnp.float32)
    for i, stat in enumerate(stats):
        block = jnp.where(row == i, jnp.broadcast_to(stat, block.shape), block)
    out_ref[pair, rows:, :] = block.astype(jnp.bfloat16)


def get_message(ref, pair, head_size):
    out = ref[pair, :head_size, :].astype(jnp.float32)
    stats = ref[pair, head_size:, :].astype(jnp.float32)
    peak = stats[0:1] + stats[1:2] + stats[2:3]
    total = stats[3:4] + stats[4:5] + stats[5:6]
    return out, peak, total


def merged(a, b, scale2):
    out_a, peak_a, total_a = a
    out_b, peak_b, total_b = b
    peak = jnp.maximum(peak_a, peak_b)
    weight_a = jnp.exp2((peak_a - peak) * scale2) * total_a
    weight_b = jnp.exp2((peak_b - peak) * scale2) * total_b
    total = weight_a + weight_b
    inv = 1.0 / total
    return out_a * (weight_a * inv) + out_b * (weight_b * inv), peak, total


def global_kernel(scale2, info_ref, q_ref, k_own_ref, k_sib_ref, v_own_ref, v_sib_ref, out_ref):
    glob, width = q_ref.shape
    head_size = width // 2
    q = q_ref[...]
    doubled = jnp.concatenate([q, q], axis=0)
    row = lax.broadcasted_iota(jnp.int32, doubled.shape, 0)
    col = lax.broadcasted_iota(jnp.int32, doubled.shape, 1)
    diag = jnp.where((row < glob) == (col < head_size), doubled, jnp.zeros_like(doubled))
    s_own = dot_t(k_own_ref[...], diag)
    s_sib = dot_t(k_sib_ref[...], diag)
    peak = jnp.maximum(jnp.max(s_own, axis=0, keepdims=True), jnp.max(s_sib, axis=0, keepdims=True))
    e_own = jnp.exp2((s_own - peak) * scale2)
    e_sib = jnp.exp2((s_sib - peak) * scale2)
    total = jnp.sum(e_own, axis=0, keepdims=True) + jnp.sum(e_sib, axis=0, keepdims=True)
    contract = (((0,), (0,)), ((), ()))
    acc = lax.dot_general(
        v_own_ref[...], e_own.astype(jnp.bfloat16), contract, preferred_element_type=jnp.float32
    ) + lax.dot_general(
        v_sib_ref[...], e_sib.astype(jnp.bfloat16), contract, preferred_element_type=jnp.float32
    )
    lane = lax.broadcasted_iota(jnp.int32, (head_size, LANES), 1)
    out = jnp.where(lane < glob, acc[:head_size], acc[head_size:]) / total
    put_message(out_ref, 0, out, peak, total)


def merge_kernel(scale2, a_ref, b_ref, out_ref):
    head_size = a_ref.shape[1] - STAT_ROWS
    for pair in range(a_ref.shape[0]):
        a = get_message(a_ref, pair, head_size)
        b = get_message(b_ref, pair, head_size)
        put_message(out_ref, pair, *merged(a, b, scale2))


def final_kernel(scale2, info_ref, a_ref, b_ref, w_ref, pos_ref, win_ref, out_ref):
    pairs = a_ref.shape[0]
    head_size = a_ref.shape[1] - STAT_ROWS
    glob = pos_ref.shape[0]
    lane = lax.broadcasted_iota(jnp.int32, (head_size, LANES), 1)
    lin = jnp.zeros((1, LANES), jnp.float32)
    sq = jnp.zeros((1, LANES), jnp.float32)
    for pair in range(pairs):
        a = get_message(a_ref, pair, head_size)
        b = get_message(b_ref, pair, head_size)
        out, _, _ = merged(a, b, scale2)
        w = jnp.where(lane < glob, w_ref[:, 2 * pair : 2 * pair + 1], w_ref[:, 2 * pair + 1 : 2 * pair + 2])
        lin = lin + jnp.sum(out * w, axis=0, keepdims=True)
        sq = sq + jnp.sum(out * out, axis=0, keepdims=True)
    lin = lin + pltpu.roll(lin, glob, 1)
    sq = sq + pltpu.roll(sq, glob, 1)
    parts = [p.astype(jnp.float32) for p in (*pieces(lin), *pieces(sq))] + [jnp.ones((1, LANES), jnp.float32)]
    row = lax.broadcasted_iota(jnp.int32, (16, LANES), 0)
    table = jnp.zeros((16, LANES), jnp.float32)
    for i, part in enumerate(parts):
        table = jnp.where(row == i, jnp.broadcast_to(part, table.shape), table)
    table = table.astype(jnp.bfloat16)[:, :glob]
    pos = pos_ref[...]
    n_pairs = win_ref.shape[1]
    base = info_ref[1]
    for j in range(n_pairs):
        token = base + j * LANES + lax.broadcasted_iota(jnp.int32, (glob, LANES), 1)
        hit = jnp.where(pos == token, 1.0, 0.0).astype(jnp.bfloat16)
        placed = dot_n(table, hit)
        is_glob = placed[6:7] > 0.5
        out_ref[j // (n_pairs // CORES), 0:1, (j % (n_pairs // CORES)) * LANES : (j % (n_pairs // CORES) + 1) * LANES] = (
            jnp.where(is_glob, placed[0:1] + placed[1:2] + placed[2:3], win_ref[0, j : j + 1, :])
        )
        out_ref[j // (n_pairs // CORES), 1:2, (j % (n_pairs // CORES)) * LANES : (j % (n_pairs // CORES) + 1) * LANES] = (
            jnp.where(is_glob, placed[3:4] + placed[4:5] + placed[5:6], win_ref[1, j : j + 1, :])
        )


def window_kernel(
    scale2,
    info_ref,
    q_own_ref,
    q_sib_ref,
    k_own_ref,
    k_sib_ref,
    v_own_ref,
    v_sib_ref,
    k_low_ref,
    k_high_ref,
    v_low_ref,
    v_high_ref,
    kg_ref,
    vg_ref,
    w_ref,
    pos_ref,
    out_ref,
    q_all,
    k_all,
    v_all,
    bias,
):
    step = pl.program_id(0)
    rows, width = q_own_ref.shape
    glob = kg_ref.shape[0]
    head_size = LANES
    n_pairs = CORES * rows // LANES
    core = info_ref[0]
    base = info_ref[1]
    lane = lax.broadcasted_iota(jnp.int32, (BLK, LANES), 1)
    left = lane < BLK

    @pl.when(step == 0)
    def _():
        out_ref[...] = jnp.zeros_like(out_ref)
        glob_block = pos_ref[...] // BLK
        for j in range(n_pairs):
            block = (base + j * LANES) // BLK + lax.broadcasted_iota(jnp.int32, (glob, LANES), 1) // BLK
            bias[j] = jnp.where(jnp.abs(glob_block - block) > 1, 0.0, NEG)

    own = pl.multiple_of(core * rows, BLK)
    sib = pl.multiple_of((1 - core) * rows, BLK)
    q_all[pl.ds(own, rows), :] = q_own_ref[...]
    q_all[pl.ds(sib, rows), :] = q_sib_ref[...]
    k_all[pl.ds(pl.multiple_of(own + BLK, BLK), rows), :] = k_own_ref[...]
    k_all[pl.ds(pl.multiple_of(sib + BLK, BLK), rows), :] = k_sib_ref[...]
    k_all[:BLK, :] = k_low_ref[...]
    k_all[BLK + CORES * rows :, :] = k_high_ref[...]
    v_all[pl.ds(pl.multiple_of(own + BLK, BLK), rows), :] = v_own_ref[...]
    v_all[pl.ds(pl.multiple_of(sib + BLK, BLK), rows), :] = v_sib_ref[...]
    v_all[:BLK, :] = v_low_ref[...]
    v_all[BLK + CORES * rows :, :] = v_high_ref[...]
    first_bias = jnp.where(left & (info_ref[2] == 1), NEG, 0.0)
    last_bias = jnp.where((~left) & (info_ref[3] == 1), NEG, 0.0)
    for head in range(width // head_size):
        cols = slice(head * head_size, (head + 1) * head_size)
        v_t = jnp.transpose(v_all[:, cols])
        vg_t = jnp.transpose(vg_ref[:, cols])
        kg = kg_ref[:, cols]
        w = jnp.broadcast_to(w_ref[0, :, head : head + 1], (head_size, LANES))
        for j in range(n_pairs):
            q = q_all[j * LANES : (j + 1) * LANES, cols]
            near = dot_t(k_all[j * LANES : (j + 2) * LANES, cols], q)
            far = dot_t(kg, q) + bias[j]
            ends = jnp.where(left, near[:BLK], near[3 * BLK :])
            if j == 0:
                ends = ends + first_bias
            if j == n_pairs - 1:
                ends = ends + last_bias
            mid = near[BLK : 3 * BLK]
            peak = jnp.max(jnp.maximum(jnp.maximum(ends, far), jnp.maximum(mid[:BLK], mid[BLK:])), axis=0, keepdims=True)
            e_ends = jnp.exp2((ends - peak) * scale2)
            e_mid = jnp.exp2((mid - peak) * scale2)
            e_far = jnp.exp2((far - peak) * scale2)
            total = jnp.sum(e_ends + e_far + e_mid[:BLK] + e_mid[BLK:], axis=0, keepdims=True)
            zero = jnp.zeros_like(e_ends)
            weights = jnp.concatenate(
                [jnp.where(left, e_ends, zero), e_mid, jnp.where(left, zero, e_ends)], axis=0
            ).astype(jnp.bfloat16)
            acc = dot_n(v_t[:, j * LANES : (j + 2) * LANES], weights) + dot_n(vg_t, e_far.astype(jnp.bfloat16))
            inv = 1.0 / total
            out_ref[0, j : j + 1, :] += jnp.sum(acc * w, axis=0, keepdims=True) * inv
            out_ref[1, j : j + 1, :] += jnp.sum(acc * acc, axis=0, keepdims=True) * (inv * inv)


def on_device(queries, keys, values, global_positions, score_weight):
    rows, model_width = queries.shape
    head_size = model_width // HEADS
    half = model_width // CORES
    half_heads = HEADS // CORES
    glob = global_positions.shape[0]
    seq_index = lax.axis_index("seq")
    seq_count = lax.axis_size("seq")
    chips = seq_count // CORES
    core = seq_index % CORES
    chip = seq_index // CORES
    scale2 = head_size ** (-0.5) * LOG2E
    bf16 = jnp.bfloat16
    f32 = jnp.float32

    def swap(x, mask):
        return lax.ppermute(x, "seq", [(i, i ^ mask) for i in range(seq_count)])

    def columns(x, which):
        return lax.dynamic_slice_in_dim(x, which * half, half, axis=1)

    row_ids = seq_index * rows + jnp.arange(rows, dtype=jnp.int32)
    select = (global_positions[:, None] == row_ids[None, :]).astype(bf16)
    chosen = [jnp.dot(select, x, preferred_element_type=f32).astype(bf16) for x in (queries, keys, values)]
    sib_sel = swap(jnp.concatenate([columns(x, 1 - core) for x in chosen], axis=0), 1)
    own_sel = jnp.concatenate([columns(x, core) for x in chosen], axis=0)
    chip_sel = own_sel + sib_sel
    q_glob = chip_sel[:glob]
    kv_glob = chip_sel[glob:]

    q_sib = swap(columns(queries, 1 - core), 1)
    kv_sib = swap(jnp.concatenate([columns(keys, 1 - core), columns(values, 1 - core)], axis=0), 1)

    for r in range(1, int(math.log2(chips)) + 1):
        q_glob = q_glob + swap(q_glob, 1 << r)
    for r in range(1, int(math.log2(chips)) + 1):
        kv_glob = kv_glob + swap(kv_glob, 1 << r)

    k_mine = columns(keys, core)
    v_mine = columns(values, core)
    k_sib, v_sib = kv_sib[:rows], kv_sib[rows:]
    is_low = core == 0
    top = jnp.concatenate(
        [jnp.where(is_low, k_mine[:BLK], k_sib[:BLK]), jnp.where(is_low, v_mine[:BLK], v_sib[:BLK])], axis=0
    )
    bottom = jnp.concatenate(
        [jnp.where(is_low, k_sib[-BLK:], k_mine[-BLK:]), jnp.where(is_low, v_sib[-BLK:], v_mine[-BLK:])], axis=0
    )
    low = lax.ppermute(bottom, "seq", [(i, i + CORES) for i in range(seq_count - CORES)])
    high = lax.ppermute(top, "seq", [(i + CORES, i) for i in range(seq_count - CORES)])

    info = jnp.stack(
        [core, chip * (CORES * rows), (chip == 0).astype(jnp.int32), (chip == chips - 1).astype(jnp.int32)]
    ).astype(jnp.int32)
    pair_width = 2 * head_size
    n_steps = half // pair_width
    own_spec = pl.BlockSpec((rows, pair_width), lambda p, info: (0, info[0] * n_steps + p))

    def part_spec(count, block=0):
        return pl.BlockSpec((count, pair_width), lambda p, info: (block, p))

    message = pl.pallas_call(
        functools.partial(global_kernel, scale2),
        grid_spec=pltpu.PrefetchScalarGridSpec(
            num_scalar_prefetch=1,
            grid=(n_steps,),
            in_specs=[part_spec(glob), own_spec, part_spec(rows), own_spec, part_spec(rows, 1)],
            out_specs=pl.BlockSpec((1, head_size + STAT_ROWS, LANES), lambda p, info: (p, 0, 0)),
        ),
        out_shape=jax.ShapeDtypeStruct((n_steps, head_size + STAT_ROWS, LANES), bf16),
        compiler_params=pltpu.CompilerParams(vmem_limit_bytes=16 * 1024 * 1024),
        name="global_partial",
    )(info, q_glob, keys, kv_sib, values, kv_sib)

    rounds = int(math.log2(chips))
    for r in range(1, rounds):
        message = pl.pallas_call(
            functools.partial(merge_kernel, scale2),
            out_shape=jax.ShapeDtypeStruct(message.shape, bf16),
            name="merge_partial",
        )(message, swap(message, 1 << r))
    message_far = swap(message, 1 << rounds)

    weight_cols = lax.dynamic_slice_in_dim(score_weight.reshape(HEADS, head_size), core * half_heads, half_heads, 0)
    weight_cols = weight_cols.reshape(n_steps, 2, head_size)
    positions = global_positions.reshape(glob, 1)
    n_pairs = CORES * rows // LANES
    whole = pl.BlockSpec((glob, 1), lambda p, info: (0, 0))
    window = pl.pallas_call(
        functools.partial(window_kernel, scale2),
        grid_spec=pltpu.PrefetchScalarGridSpec(
            num_scalar_prefetch=1,
            grid=(n_steps,),
            in_specs=[
                own_spec,
                part_spec(rows),
                own_spec,
                part_spec(rows),
                own_spec,
                part_spec(rows, 1),
                part_spec(BLK),
                part_spec(BLK),
                part_spec(BLK, 1),
                part_spec(BLK, 1),
                part_spec(glob),
                part_spec(glob, 1),
                pl.BlockSpec((1, head_size, 2), lambda p, info: (p, 0, 0)),
                whole,
            ],
            out_specs=pl.BlockSpec((2, n_pairs, LANES), lambda p, info: (0, 0, 0)),
            scratch_shapes=[
                pltpu.VMEM((CORES * rows, pair_width), bf16),
                pltpu.VMEM((CORES * rows + 2 * BLK, pair_width), bf16),
                pltpu.VMEM((CORES * rows + 2 * BLK, pair_width), bf16),
                pltpu.VMEM((n_pairs, glob, LANES), f32),
            ],
        ),
        out_shape=jax.ShapeDtypeStruct((2, n_pairs, LANES), f32),
        compiler_params=pltpu.CompilerParams(vmem_limit_bytes=24 * 1024 * 1024),
        name="window_attention",
    )(
        info,
        queries,
        q_sib,
        keys,
        kv_sib,
        values,
        kv_sib,
        low,
        high,
        low,
        high,
        kv_glob,
        kv_glob,
        jnp.transpose(weight_cols, (0, 2, 1)),
        positions,
    )

    vmem = pl.BlockSpec(memory_space=pltpu.VMEM)
    sums = pl.pallas_call(
        functools.partial(final_kernel, scale2),
        in_specs=[pl.BlockSpec(memory_space=pltpu.SMEM), vmem, vmem, vmem, vmem, vmem],
        out_specs=vmem,
        out_shape=jax.ShapeDtypeStruct((CORES, 2, rows), f32),
        name="place_global",
    )(info, message, message_far, jnp.transpose(weight_cols.reshape(half_heads, head_size)), positions, window)
    mine = lax.dynamic_index_in_dim(sums, core, 0, keepdims=False)
    theirs = swap(lax.dynamic_index_in_dim(sums, 1 - core, 0, keepdims=False), 1)
    both = mine + theirs
    return both[0] * lax.rsqrt(both[1] * (1.0 / model_width) + 1e-06)


def solution(mesh):
    placed = (
        P(("doc", "seq"), None),
        P(("doc", "seq"), None),
        P(("doc", "seq"), None),
        P("doc"),
        P(),
    )
    return jax.shard_map(
        on_device, mesh=mesh, in_specs=placed, out_specs=P(("doc", "seq")), check_vma=False
    )
```

time: 180 us -> 75.6 us (0.42)
  waiting for transfers between devices: 59.4 us -> 15.3 us
  other arithmetic: 41.9 us -> 8.21 us
  blocking collectives: 28 us -> 0 us
  Pallas kernels: 0 us -> 21.1 us
  between operations: 13.7 us -> 0.2 us
  matrix products: 15.1 us -> 2.72 us
  starting transfers between devices: 4.48 us -> 12.4 us
    psum x2 -> x0, waiting for transfers between devices: 59.4 us -> none  [the longest x1 59.4 us: on_device(): lax.psum(glob_parts[0], 'seq').astype(jnp.float32)]
    sub x1 -> x0, other arithmetic: 36.3 us -> none  [on_device(): exp_scores = jnp.exp(scores - row_max)]
    pallas_call x0 -> x4, Pallas kernels: none -> 21.1 us  [the longest x1 13.5 us: on_device(): pl.pallas_call(functools.partial(window_kernel, scale2), grid_spec=pltpu....]
    ppermute x2 -> x12, waiting for transfers between devices: 0.01 us -> 15.3 us  [the longest x10 14.9 us: swap(): return lax.ppermute(x, 'seq', [(i, i ^ mask) for i in range(seq_count)])]
    psum x1 -> x0, blocking collectives: 14 us -> none  [on_device(): acc_whole, total_whole = lax.psum((scaled_acc, seg_total * rescale), 'seq')]
    pmax x1 -> x0, blocking collectives: 13.9 us -> none  [on_device(): top_peak = lax.pmax(seg_peak, 'seq')]
    dot_general x14 -> x3, matrix products: 15.1 us -> 2.72 us  [on_device(): jnp.dot(select, x, preferred_element_type=f32).astype(bf16)]
    ppermute x2 -> x12, starting transfers between devices: 4.44 us -> 12.4 us  [the longest x10 8.8 us: swap(): return lax.ppermute(x, 'seq', [(i, i ^ mask) for i in range(seq_count)])]
  transfers between devices with their start and end apart: 4 -> 12, of which waited for: 1 -> 6; matrix products, arithmetic and copies ran while one was open for 36% -> 19% of each run, Pallas kernels for 0% -> 25%
where the time goes in v1:
time: 75.6 us; the launch traced here: 75.1 us
  Pallas kernels  21.1 us (28%)
  waiting for transfers between devices  15.3 us (20%)
  local copies, waits for them, and re-layouts  15.2 us (20%)
  starting transfers between devices  12.4 us (16%)
  other arithmetic  8.21 us (11%)
  matrix products  2.72 us (4%)
    ppermute x10, waiting for transfers between devices, swap(): return lax.ppermute(x, 'seq', [(i, i ^ mask) for i in range(seq_count)])  14.9 us
    pallas_call x1, Pallas kernels, on_device(): pl.pallas_call(functools.partial(window_kernel, scale2), grid_spec=pltpu....  13.5 us
    ppermute x10, starting transfers between devices, swap(): return lax.ppermute(x, 'seq', [(i, i ^ mask) for i in range(seq_count)])  8.8 us
    unnamed x29, local copies, waits for them, and re-layouts  7.52 us
    dynamic_slice x4, local copies, waits for them, and re-layouts, columns(): return lax.dynamic_slice_in_dim(x, which * half, half, axis=1)  4.62 us
    pallas_call x1, Pallas kernels, on_device(): pl.pallas_call(functools.partial(global_kernel, scale2), grid_spec=pltpu....  3.74 us
    add x2, other arithmetic, on_device(): kv_glob = kv_glob + swap(kv_glob, 1 << r)  2.79 us
    dot_general x3, matrix products, on_device(): jnp.dot(select, x, preferred_element_type=f32).astype(bf16)  2.72 us
  transfers between devices with their start and end apart: 12, of which 6 were waited for; matrix products, arithmetic and copies ran while one was open for 19% of the time, Pallas kernels for 25%

profile of v1, /device:TPU:0, one launch (start us, length us, event | category | flops | bytes accessed | tf_op | source)
XLA Modules:
  0.0 75.1 jit_solution(16579995510742740926)
XLA Ops:
  0.0 1.5 %constant_dynamic-slice_fusion.4 = (bf16[384,1024]{1,0:T(8,128)(2,1)S(1)}, bf16[384,1024]{1,0:T(8,128)(2,1)S(1)}) fusion(bf16[384,2048]{1,0:T(8,128)(2,1)} %v_own_ref.3, s32[]{:T(128)S(6)} %select_n.59, bf16[384,2048]{1,0:T(8,128)(2,1)} %k_own_ref.3), kind=kLoop, calls=%fused_computation.25 | loop fusion | bytes 3145732 | tf_op jit(solution)/shard_map/dynamic_slice | solution.py:242
  1.5 1.3 %pad_maximum_fusion = bf16[768,1024]{1,0:T(8,128)(2,1)} fusion(bf16[384,1024]{1,0:T(8,128)(2,1)S(1)} %get-tuple-element.19, bf16[384,1024]{1,0:T(8,128)(2,1)S(1)} %get-tuple-element.20), kind=kLoop, calls=%fused_computation.3 | loop fusion | flops 3145728 | bytes 3145728 | tf_op jit(solution)/shard_map/concatenate | solution.py:254
  2.8 0.5 collective-permute-start.3
  3.3 0.2 copy-done.1
  3.5 0.4 convolution_convert_fusion
  3.9 0.8 %copy-done.2 = bf16[384,2048]{1,0:T(8,128)(2,1)S(1)} copy-done((bf16[384,2048]{1,0:T(8,128)(2,1)S(1)}, bf16[384,2048]{1,0:T(8,128)(2,1)}, u32[]{:S(2)}) %copy-start.2) | copy-done | bytes 1572888
  4.7 1.1 %convolution_convert_fusion.1 = bf16[64,2048]{1,0:T(8,128)(2,1)} fusion(bf16[384,2048]{1,0:T(8,128)(2,1)S(1)} %copy-done.2, s32[384]{0:T(512)S(1)} %iota_add_fusion, s32[64]{0:T(128)S(1)} %copy-done.13), kind=kOutput, calls=%fused_computation.1 | convolution fusion | flops 100818944 | bytes 1836800 | tf_op jit(solution)/shard_map/dot_general | solution.py:246
  5.9 1.1 %convolution_convert_fusion.2 = bf16[64,2048]{1,0:T(8,128)(2,1)} fusion(bf16[384,2048]{1,0:T(8,128)(2,1)S(1)} %copy-done.5, s32[384]{0:T(512)S(1)} %iota_add_fusion, s32[64]{0:T(128)S(1)} %copy-done.13), kind=kOutput, calls=%fused_computation.2 | convolution fusion | flops 100818944 | bytes 1836800 | tf_op jit(solution)/shard_map/dot_general | solution.py:246
  7.0 1.0 %constant_dynamic-slice_fusion.9 = (bf16[64,1024]{1,0:T(8,128)(2,1)S(1)}, bf16[64,1024]{1,0:T(8,128)(2,1)S(1)}, bf16[64,1024]{1,0:T(8,128)(2,1)S(1)}, bf16[64,1024]{1,0:T(8,128)(2,1)S(1)}) fusion(bf16[64,2048]{1,0:T(8,128)(2,1)S(1)} %convolution_convert_fusion, s32[]{:T(128)S(6)} %select_n.58, s32[]{:T(128)S(6)} %select_n.59, ...), kind=kLoop, calls=%fused_computation.30 | loop fusion | bytes 1048584 | tf_op jit(solution)/shard_map/dynamic_slice | solution.py:242
  8.1 1.1 %constant_dynamic-slice_fusion.11 = (bf16[64,1024]{1,0:T(8,128)(2,1)S(1)}, bf16[64,1024]{1,0:T(8,128)(2,1)S(1)}) fusion(bf16[64,2048]{1,0:T(8,128)(2,1)} %convolution_convert_fusion.2, s32[]{:T(128)S(6)} %select_n.58, s32[]{:T(128)S(6)} %select_n.59), kind=kLoop, calls=%fused_computation.32 | loop fusion | bytes 524296 | tf_op jit(solution)/shard_map/dynamic_slice | solution.py:242
  9.2 0.2 collective-permute-start
  9.4 1.6 %collective-permute-done = bf16[192,1024]{1,0:T(8,128)(2,1)S(1)} collective-permute-done((bf16[192,1024]{1,0:T(8,128)(2,1)S(1)}, bf16[192,1024]{1,0:T(8,128)(2,1)S(1)}, u32[]{:S(2)}, u32[]{:S(2)}) %collective-permute-start) | collective-permute-done | bytes 393248 | tf_op jit(solution)/shard_map/ppermute | solution.py:239
  11.1 0.7 slice.54
  11.8 2.7 %collective-permute-start.1 = (bf16[64,1024]{1,0:T(8,128)(2,1)}, bf16[64,1024]{1,0:T(8,128)(2,1)}, u32[]{:S(2)}, u32[]{:S(2)}) collective-permute-start(bf16[64,1024]{1,0:T(8,128)(2,1)} %slice.54), channel_id=1, source_target_pairs={{0,2},{1,3},{2,0},{3,1},{4,6},{5,7},{6,4},{7,5},{8,10},{9,11},{10,... | collective-permute-start | bytes 393224 | tf_op jit(solution)/shard_map/ppermute | solution.py:239
  14.5 1.0 %constant_dynamic-slice_fusion.2 = bf16[384,1024]{1,0:T(8,128)(2,1)} fusion(bf16[384,2048]{1,0:T(8,128)(2,1)S(1)} %copy-done.6, s32[]{:T(128)S(6)} %select_n.59), kind=kLoop, calls=%fused_computation.23 | loop fusion | bytes 1572868 | tf_op jit(solution)/shard_map/dynamic_slice | solution.py:242
  15.5 0.7 slice.59
  16.3 0.3 collective-permute-start.9
  16.6 2.2 %collective-permute-done.1 = bf16[64,1024]{1,0:T(8,128)(2,1)} collective-permute-done((bf16[64,1024]{1,0:T(8,128)(2,1)}, bf16[64,1024]{1,0:T(8,128)(2,1)}, u32[]{:S(2)}, u32[]{:S(2)}) %collective-permute-start.1) | collective-permute-done | bytes 131104 | tf_op jit(solution)/shard_map/ppermute | solution.py:239
  18.8 0.9 %slice_add_fusion = bf16[64,1024]{1,0:T(8,128)(2,1)S(1)} fusion(bf16[64,1024]{1,0:T(8,128)(2,1)} %collective-permute-done.1, bf16[192,1024]{1,0:T(8,128)(2,1)S(1)} %maximum_add_fusion), kind=kLoop, calls=%fused_computation.43 | loop fusion | flops 65536 | bytes 393216 | tf_op jit(solution)/shard_map/add | solution.py:257
  19.7 2.8 %collective-permute-start.2 = (bf16[64,1024]{1,0:T(8,128)(2,1)S(1)}, bf16[64,1024]{1,0:T(8,128)(2,1)S(1)}, u32[]{:S(2)}, u32[]{:S(2)}) collective-permute-start(bf16[64,1024]{1,0:T(8,128)(2,1)S(1)} %slice_add_fusion), channel_id=1, source_target_pairs={{0,4},{1,5},{2,6},{3,7},{4,0},{5,1},{6,2},{7,3},{8,12},{9,13},{10,... | collective-permute-start | bytes 393224 | tf_op jit(solution)/shard_map/ppermute | solution.py:239
  22.6 5.5 %collective-permute-done.9 = bf16[128,1024]{1,0:T(8,128)(2,1)} collective-permute-done((bf16[128,1024]{1,0:T(8,128)(2,1)}, bf16[128,1024]{1,0:T(8,128)(2,1)}, u32[]{:S(2)}, u32[]{:S(2)}) %collective-permute-start.9) | collective-permute-done | bytes 262176 | tf_op jit(solution)/shard_map/ppermute | solution.py:239
  28.1 1.7 %slice_add_fusion.1 = bf16[128,1024]{1,0:T(8,128)(2,1)} fusion(bf16[128,1024]{1,0:T(8,128)(2,1)} %collective-permute-done.9, bf16[192,1024]{1,0:T(8,128)(2,1)S(1)} %maximum_add_fusion), kind=kLoop, calls=%fused_computation.44 | loop fusion | flops 131072 | bytes 786432 | tf_op jit(solution)/shard_map/add | solution.py:259
  29.8 0.2 collective-permute-start.10
  30.1 1.4 %copy-done.3 = bf16[384,2048]{1,0:T(8,128)(2,1)S(1)} copy-done((bf16[384,2048]{1,0:T(8,128)(2,1)S(1)}, bf16[384,2048]{1,0:T(8,128)(2,1)}, u32[]{:S(2)}) %copy-start.3) | copy-done | bytes 1572888
  31.5 3.7 %global_partial.1.a_ref = bf16[4,144,128]{2,1,0:T(8,128)(2,1)S(1)} custom-call(s32[4]{0:T(128)S(1)} %pad_add_fusion.info_ref, bf16[64,1024]{1,0:T(8,128)(2,1)S(1)} %add.73.q_ref, bf16[384,2048]{1,0:T(8,128)(2,1)S(1)} %copy-done.3, bf16[768,1024]{1,0:T(8,128)(2,1)S(1)} %collective-permute-done.3.k_sib_ref.v_sib_ref, bf16[384,2048]{1,0:T(8,128)(2,1)S(1)} %copy-done.1, ...), custom_call_target="tpu_custom_call" | custom-call | tf_op jit(solution)/shard_map/global_partial/pallas_call | solution.py:284
  35.2 1.9 %collective-permute-start.4 = (bf16[4,144,128]{2,1,0:T(8,128)(2,1)S(1)}, bf16[4,144,128]{2,1,0:T(8,128)(2,1)}, u32[]{:S(2)}, u32[]{:S(2)}) collective-permute-start(bf16[4,144,128]{2,1,0:T(8,128)(2,1)S(1)} %global_partial.1.a_ref), channel_id=1, source_target_pairs={{0,2},{1,3},{2,0},{3,1},{4,6},{5,7},{6,4},{7,5},{8,10},{9,11},{10,... | collective-permute-start | bytes 442376 | tf_op jit(solution)/shard_map/ppermute | solution.py:239
  37.1 0.2 slice_select_fusion.1
  37.3 0.7 pad_maximum_fusion.2
  38.0 2.3 %collective-permute-start.7 = (bf16[128,1024]{1,0:T(8,128)(2,1)}, bf16[128,1024]{1,0:T(8,128)(2,1)S(1)}, u32[]{:S(2)}, u32[]{:S(2)}) collective-permute-start(bf16[128,1024]{1,0:T(8,128)(2,1)} %pad_maximum_fusion.2), channel_id=1, source_target_pairs={{0,2},{1,3},{2,4},{3,5},{4,6},{5,7},{8,10},{9,11},{10,12},{11,13},... | collective-permute-start | bytes 786440 | tf_op jit(solution)/shard_map/ppermute | solution.py:271
  40.3 0.7 pad_maximum_fusion.3
  41.0 1.3 %collective-permute-start.8 = (bf16[128,1024]{1,0:T(8,128)(2,1)}, bf16[128,1024]{1,0:T(8,128)(2,1)}, u32[]{:S(2)}, u32[]{:S(2)}) collective-permute-start(bf16[128,1024]{1,0:T(8,128)(2,1)} %pad_maximum_fusion.3), channel_id=1, source_target_pairs={{2,0},{3,1},{4,2},{5,3},{6,4},{7,5},{10,8},{11,9},{12,10},{13,11},... | collective-permute-start | bytes 786440 | tf_op jit(solution)/shard_map/ppermute | solution.py:272
  42.3 4.4 %collective-permute-done.4.b_ref = bf16[4,144,128]{2,1,0:T(8,128)(2,1)} collective-permute-done((bf16[4,144,128]{2,1,0:T(8,128)(2,1)S(1)}, bf16[4,144,128]{2,1,0:T(8,128)(2,1)}, u32[]{:S(2)}, u32[]{:S(2)}) %collective-permute-start.4) | collective-permute-done | bytes 147488 | tf_op jit(solution)/shard_map/ppermute | solution.py:239
  46.8 1.7 %merge_partial.1.a_ref = bf16[4,144,128]{2,1,0:T(8,128)(2,1)} custom-call(bf16[4,144,128]{2,1,0:T(8,128)(2,1)} %copy-done.9, bf16[4,144,128]{2,1,0:T(8,128)(2,1)} %collective-permute-done.4.b_ref), custom_call_target="tpu_custom_call" | custom-call | tf_op jit(solution)/shard_map/merge_partial/pallas_call | solution.py:299
  48.5 0.2 collective-permute-start.5
  48.7 0.7 copy.13
  49.5 0.9 %copy.10 = f32[4,2,128]{1,2,0:T(8,128)} copy(f32[4,2,128]{2,1,0:T(2,128)S(1)} %bitcast.21) | data formatting | bytes 8192 | tf_op jit(solution)/shard_map/reshape | solution.py:307
  50.4 1.1 %add.76.kg_ref.vg_ref = bf16[128,1024]{1,0:T(8,128)(2,1)S(1)} add(bf16[128,1024]{1,0:T(8,128)(2,1)} %slice_add_fusion.1, bf16[128,1024]{1,0:T(8,128)(2,1)} %collective-permute-done.10) | non-fusion elementwise | flops 131072 | bytes 786432 | tf_op jit(solution)/shard_map/add | solution.py:259
  51.5 0.5 collective-permute-done.8.k_high_ref.v_high_ref
  51.9 1.4 %copy-done.4 = bf16[384,2048]{1,0:T(8,128)(2,1)S(1)} copy-done((bf16[384,2048]{1,0:T(8,128)(2,1)S(1)}, bf16[384,2048]{1,0:T(8,128)(2,1)}, u32[]{:S(2)}) %copy-start.4) | copy-done | bytes 1572888
  53.4 1.4 %copy-done.7 = bf16[384,2048]{1,0:T(8,128)(2,1)S(1)} copy-done((bf16[384,2048]{1,0:T(8,128)(2,1)S(1)}, bf16[384,2048]{1,0:T(8,128)(2,1)}, u32[]{:S(2)}) %copy-start.7) | copy-done | bytes 1572888
  54.8 0.9 %copy-done.8 = f32[4,2,128]{1,2,0:T(8,128)S(1)} copy-done((f32[4,2,128]{1,2,0:T(8,128)S(1)}, f32[4,2,128]{1,2,0:T(8,128)}, u32[]{:S(2)}) %copy-start.8) | copy-done | bytes 4120
  55.7 13.5 %window_attention.1.win_ref = f32[2,6,128]{2,1,0:T(8,128)S(1)} custom-call(s32[4]{0:T(128)S(1)} %pad_add_fusion.info_ref, bf16[384,2048]{1,0:T(8,128)(2,1)S(1)} %copy-done.7, bf16[384,1024]{1,0:T(8,128)(2,1)} %collective-permute-done.6.q_sib_ref, bf16[384,2048]{1,0:T(8,128)(2,1)S(1)} %copy-done.4, ...), custom_call_target="tpu_custom_call" | custom-call | tf_op jit(solution)/shard_map/window_attention/pallas_call | solution.py:311
  69.2 0.6 copy-done.11
  69.8 2.1 %place_global.1 = f32[2,2,384]{2,1,0:T(2,128)} custom-call(s32[4]{0:T(128)} %copy-done.12, bf16[4,144,128]{2,1,0:T(8,128)(2,1)} %merge_partial.1.a_ref, bf16[4,144,128]{2,1,0:T(8,128)(2,1)} %collective-permute-done.5.b_ref, f32[128,8]{1,0:T(8,128)} %bitcast.20, s32[64,1]{1,0:T(8,128)} %copy-done.10, f32[2,6,128]{2,1,0:T(8,128)} %copy-done.11), custom_call_target="tpu_custom_call" | custom-call | tf_op jit(solution)/shard_map/place_global/pallas_call | solution.py:362
  71.9 0.7 fusion.11
  72.6 1.2 %collective-permute-done.11 = f32[2,384]{1,0:T(2,128)S(1)} collective-permute-done((f32[2,384]{1,0:T(2,128)S(1)}, f32[2,384]{1,0:T(2,128)S(1)}, u32[]{:S(2)}, u32[]{:S(2)}) %collective-permute-start.11) | collective-permute-done | bytes 3104 | tf_op jit(solution)/shard_map/ppermute | solution.py:239
  73.8 0.7 fusion.10
  74.5 0.6 fusion.15
  (36 shorter events, 0.5 us)
Async XLA Ops:
  0.0 48.7 %copy-start = (f32[2048]{0:T(1024)S(1)}, f32[2048]{0:T(1024)}, u32[]{:S(2)}) copy-start(f32[2048]{0:T(1024)} %param.9) | copy-start | bytes 24580
  1.5 2.0 %copy-start.1 = (bf16[384,2048]{1,0:T(8,128)(2,1)S(1)}, bf16[384,2048]{1,0:T(8,128)(2,1)}, u32[]{:S(2)}) copy-start(bf16[384,2048]{1,0:T(8,128)(2,1)} %v_own_ref.3) | copy-start | bytes 4718596
  1.5 2.0 %copy-start.13 = (s32[64]{0:T(128)S(1)}, s32[64]{0:T(128)}, u32[]{:S(2)}) copy-start(s32[64]{0:T(128)} %param.8) | copy-start | bytes 772
  2.8 27.2 %collective-permute-start.3 = (bf16[768,1024]{1,0:T(8,128)(2,1)}, bf16[768,1024]{1,0:T(8,128)(2,1)S(1)}, u32[]{:S(2)}, u32[]{:S(2)}) collective-permute-start(bf16[768,1024]{1,0:T(8,128)(2,1)} %pad_maximum_fusion), channel_id=1, source_target_pairs={{0,1},{1,0},{2,3},{3,2},{4,5},{5,4},{6,7},{7,6},{8,9},{9,8},{10,11... | collective-permute-start | bytes 4718600 | tf_op jit(solution)/shard_map/ppermute | solution.py:239
  3.3 1.5 %copy-start.2 = (bf16[384,2048]{1,0:T(8,128)(2,1)S(1)}, bf16[384,2048]{1,0:T(8,128)(2,1)}, u32[]{:S(2)}) copy-start(bf16[384,2048]{1,0:T(8,128)(2,1)} %k_own_ref.3) | copy-start | bytes 4718596
  3.5 2.4 %copy-start.5 = (bf16[384,2048]{1,0:T(8,128)(2,1)S(1)}, bf16[384,2048]{1,0:T(8,128)(2,1)}, u32[]{:S(2)}) copy-start(bf16[384,2048]{1,0:T(8,128)(2,1)} %q_own_ref.1) | copy-start | bytes 4718596
  8.1 6.4 %copy-start.6 = (bf16[384,2048]{1,0:T(8,128)(2,1)S(1)}, bf16[384,2048]{1,0:T(8,128)(2,1)}, u32[]{:S(2)}) copy-start(bf16[384,2048]{1,0:T(8,128)(2,1)} %q_own_ref.1) | copy-start | bytes 4718596
  9.2 1.8 %collective-permute-start = (bf16[192,1024]{1,0:T(8,128)(2,1)S(1)}, bf16[192,1024]{1,0:T(8,128)(2,1)S(1)}, u32[]{:S(2)}, u32[]{:S(2)}) collective-permute-start(bf16[192,1024]{1,0:T(8,128)(2,1)S(1)} %pad_maximum_fusion.1), channel_id=1, source_target_pairs={{0,1},{1,0},{2,3},{3,2},{4,5},{5,4},{6,7},{7,6},{8,9},{9,8},{10,11... | collective-permute-start | bytes 1179656 | tf_op jit(solution)/shard_map/ppermute | solution.py:239
  11.8 7.0 %collective-permute-start.1 = (bf16[64,1024]{1,0:T(8,128)(2,1)}, bf16[64,1024]{1,0:T(8,128)(2,1)}, u32[]{:S(2)}, u32[]{:S(2)}) collective-permute-start(bf16[64,1024]{1,0:T(8,128)(2,1)} %slice.54), channel_id=1, source_target_pairs={{0,2},{1,3},{2,0},{3,1},{4,6},{5,7},{6,4},{7,5},{8,10},{9,11},{10,... | collective-permute-start | bytes 393224 | tf_op jit(solution)/shard_map/ppermute | solution.py:239
  15.5 36.0 %collective-permute-start.6 = (bf16[384,1024]{1,0:T(8,128)(2,1)}, bf16[384,1024]{1,0:T(8,128)(2,1)}, u32[]{:S(2)}, u32[]{:S(2)}) collective-permute-start(bf16[384,1024]{1,0:T(8,128)(2,1)} %constant_dynamic-slice_fusion.2), channel_id=1, source_target_pairs={{0,1},{1,0},{2,3},{3,2},{4,5},{5,4},{6,7},{7,6},{8,9},{9,8},{10,11... | collective-permute-start | bytes 2359304 | tf_op jit(solution)/shard_map/ppermute | solution.py:239
  16.3 11.8 %collective-permute-start.9 = (bf16[128,1024]{1,0:T(8,128)(2,1)}, bf16[128,1024]{1,0:T(8,128)(2,1)}, u32[]{:S(2)}, u32[]{:S(2)}) collective-permute-start(bf16[128,1024]{1,0:T(8,128)(2,1)} %slice.59), channel_id=1, source_target_pairs={{0,2},{1,3},{2,0},{3,1},{4,6},{5,7},{6,4},{7,5},{8,10},{9,11},{10,... | collective-permute-start | bytes 786440 | tf_op jit(solution)/shard_map/ppermute | solution.py:239
  16.6 35.3 %copy-start.12 = (s32[4]{0:T(128)}, s32[4]{0:T(128)S(1)}, u32[]{:S(2)}) copy-start(s32[4]{0:T(128)S(1)} %pad_add_fusion.info_ref) | copy-start | bytes 52
  19.7 10.3 %collective-permute-start.2 = (bf16[64,1024]{1,0:T(8,128)(2,1)S(1)}, bf16[64,1024]{1,0:T(8,128)(2,1)S(1)}, u32[]{:S(2)}, u32[]{:S(2)}) collective-permute-start(bf16[64,1024]{1,0:T(8,128)(2,1)S(1)} %slice_add_fusion), channel_id=1, source_target_pairs={{0,4},{1,5},{2,6},{3,7},{4,0},{5,1},{6,2},{7,3},{8,12},{9,13},{10,... | collective-permute-start | bytes 393224 | tf_op jit(solution)/shard_map/ppermute | solution.py:239
  29.8 20.6 %collective-permute-start.10 = (bf16[128,1024]{1,0:T(8,128)(2,1)}, bf16[128,1024]{1,0:T(8,128)(2,1)}, u32[]{:S(2)}, u32[]{:S(2)}) collective-permute-start(bf16[128,1024]{1,0:T(8,128)(2,1)} %slice_add_fusion.1), channel_id=1, source_target_pairs={{0,4},{1,5},{2,6},{3,7},{4,0},{5,1},{6,2},{7,3},{8,12},{9,13},{10,... | collective-permute-start | bytes 786440 | tf_op jit(solution)/shard_map/ppermute | solution.py:239
  30.0 1.4 %copy-start.3 = (bf16[384,2048]{1,0:T(8,128)(2,1)S(1)}, bf16[384,2048]{1,0:T(8,128)(2,1)}, u32[]{:S(2)}) copy-start(bf16[384,2048]{1,0:T(8,128)(2,1)} %k_own_ref.3) | copy-start | bytes 4718596
  35.2 2.1 %copy-start.9 = (bf16[4,144,128]{2,1,0:T(8,128)(2,1)}, bf16[4,144,128]{2,1,0:T(8,128)(2,1)S(1)}, u32[]{:S(2)}) copy-start(bf16[4,144,128]{2,1,0:T(8,128)(2,1)S(1)} %global_partial.1.a_ref) | copy-start | bytes 442372
  35.2 11.5 %collective-permute-start.4 = (bf16[4,144,128]{2,1,0:T(8,128)(2,1)S(1)}, bf16[4,144,128]{2,1,0:T(8,128)(2,1)}, u32[]{:S(2)}, u32[]{:S(2)}) collective-permute-start(bf16[4,144,128]{2,1,0:T(8,128)(2,1)S(1)} %global_partial.1.a_ref), channel_id=1, source_target_pairs={{0,2},{1,3},{2,0},{3,1},{4,6},{5,7},{6,4},{7,5},{8,10},{9,11},{10,... | collective-permute-start | bytes 442376 | tf_op jit(solution)/shard_map/ppermute | solution.py:239
  38.0 13.4 %collective-permute-start.7 = (bf16[128,1024]{1,0:T(8,128)(2,1)}, bf16[128,1024]{1,0:T(8,128)(2,1)S(1)}, u32[]{:S(2)}, u32[]{:S(2)}) collective-permute-start(bf16[128,1024]{1,0:T(8,128)(2,1)} %pad_maximum_fusion.2), channel_id=1, source_target_pairs={{0,2},{1,3},{2,4},{3,5},{4,6},{5,7},{8,10},{9,11},{10,12},{11,13},... | collective-permute-start | bytes 786440 | tf_op jit(solution)/shard_map/ppermute | solution.py:271
  41.0 10.9 %collective-permute-start.8 = (bf16[128,1024]{1,0:T(8,128)(2,1)}, bf16[128,1024]{1,0:T(8,128)(2,1)}, u32[]{:S(2)}, u32[]{:S(2)}) collective-permute-start(bf16[128,1024]{1,0:T(8,128)(2,1)} %pad_maximum_fusion.3), channel_id=1, source_target_pairs={{2,0},{3,1},{4,2},{5,3},{6,4},{7,5},{10,8},{11,9},{12,10},{13,11},... | collective-permute-start | bytes 786440 | tf_op jit(solution)/shard_map/ppermute | solution.py:272
  48.5 21.3 %collective-permute-start.5 = (bf16[4,144,128]{2,1,0:T(8,128)(2,1)}, bf16[4,144,128]{2,1,0:T(8,128)(2,1)}, u32[]{:S(2)}, u32[]{:S(2)}) collective-permute-start(bf16[4,144,128]{2,1,0:T(8,128)(2,1)} %merge_partial.1.a_ref), channel_id=1, source_target_pairs={{0,4},{1,5},{2,6},{3,7},{4,0},{5,1},{6,2},{7,3},{8,12},{9,13},{10,... | collective-permute-start | bytes 442376 | tf_op jit(solution)/shard_map/ppermute | solution.py:239
  49.5 19.7 %copy-start.10 = (s32[64,1]{1,0:T(8,128)}, s32[64,1]{1,0:T(8,128)S(1)}, u32[]{:S(2)}) copy-start(s32[64,1]{1,0:T(8,128)S(1)} %copy.12.pos_ref) | copy-start | bytes 772
  51.9 1.4 %copy-start.4 = (bf16[384,2048]{1,0:T(8,128)(2,1)S(1)}, bf16[384,2048]{1,0:T(8,128)(2,1)}, u32[]{:S(2)}) copy-start(bf16[384,2048]{1,0:T(8,128)(2,1)} %k_own_ref.3) | copy-start | bytes 4718596
  53.3 1.4 %copy-start.7 = (bf16[384,2048]{1,0:T(8,128)(2,1)S(1)}, bf16[384,2048]{1,0:T(8,128)(2,1)}, u32[]{:S(2)}) copy-start(bf16[384,2048]{1,0:T(8,128)(2,1)} %q_own_ref.1) | copy-start | bytes 4718596
  54.8 0.9 %copy-start.8 = (f32[4,2,128]{1,2,0:T(8,128)S(1)}, f32[4,2,128]{1,2,0:T(8,128)}, u32[]{:S(2)}) copy-start(f32[4,2,128]{1,2,0:T(8,128)} %copy.10) | copy-start | bytes 12292
  69.2 0.6 copy-start.11
  72.6 1.2 %collective-permute-start.11 = (f32[2,384]{1,0:T(2,128)S(1)}, f32[2,384]{1,0:T(2,128)S(1)}, u32[]{:S(2)}, u32[]{:S(2)}) collective-permute-start(f32[2,384]{1,0:T(2,128)S(1)} %fusion.11), channel_id=1, source_target_pairs={{0,1},{1,0},{2,3},{3,2},{4,5},{5,4},{6,7},{7,6},{8,9},{9,8},{10,11... | collective-permute-start | bytes 9224 | tf_op jit(solution)/shard_map/ppermute | solution.py:239

commit v2 on v1

v2 whole, which is shorter than its diff:
```python
import functools
import math

import jax
import jax.numpy as jnp
from jax import lax
from jax.experimental import pallas as pl
from jax.experimental.pallas import tpu as pltpu
from jax.sharding import PartitionSpec as P

HEADS = 16
BLK = 64
CORES = 2
LANES = 128
NEG = -1e30
LOG2E = math.log2(math.e)
STAT_ROWS = 16


def pieces(x):
    hi = x.astype(jnp.bfloat16)
    rest = x - hi.astype(jnp.float32)
    mid = rest.astype(jnp.bfloat16)
    low = (rest - mid.astype(jnp.float32)).astype(jnp.bfloat16)
    return hi, mid, low


def dot_t(a, b):
    return lax.dot_general(a, b, (((1,), (1,)), ((), ())), preferred_element_type=jnp.float32)


def dot_n(a, b):
    return lax.dot_general(a, b, (((1,), (0,)), ((), ())), preferred_element_type=jnp.float32)


def put_message(out_ref, pair, out, peak, total):
    rows = out.shape[0]
    out_ref[pair, :rows, :] = out.astype(jnp.bfloat16)
    stats = [p.astype(jnp.float32) for p in (*pieces(peak), *pieces(total))]
    row = lax.broadcasted_iota(jnp.int32, (STAT_ROWS, LANES), 0)
    block = jnp.zeros((STAT_ROWS, LANES), jnp.float32)
    for i, stat in enumerate(stats):
        block = jnp.where(row == i, jnp.broadcast_to(stat, block.shape), block)
    out_ref[pair, rows:, :] = block.astype(jnp.bfloat16)


def get_message(ref, pair, head_size):
    out = ref[pair, :head_size, :].astype(jnp.float32)
    stats = ref[pair, head_size:, :].astype(jnp.float32)
    peak = stats[0:1] + stats[1:2] + stats[2:3]
    total = stats[3:4] + stats[4:5] + stats[5:6]
    return out, peak, total


def merged(a, b, scale2):
    out_a, peak_a, total_a = a
    out_b, peak_b, total_b = b
    peak = jnp.maximum(peak_a, peak_b)
    weight_a = jnp.exp2((peak_a - peak) * scale2) * total_a
    weight_b = jnp.exp2((peak_b - peak) * scale2) * total_b
    total = weight_a + weight_b
    inv = 1.0 / total
    return out_a * (weight_a * inv) + out_b * (weight_b * inv), peak, total


def device_place():
    index = lax.axis_index("seq")
    return index % CORES, index // CORES


def select_kernel(base_of, half, pos_ref, *refs):
    count = (len(refs) - 2) if len(refs) < 4 else (len(refs) - 2)
    x_refs, own_ref, sib_ref = refs[:count], refs[count], refs[count + 1]
    rows = x_refs[0].shape[0]
    glob = pos_ref.shape[1]
    core, chip = device_place()
    base = (chip * CORES + core) * rows
    row = base + lax.broadcasted_iota(jnp.int32, (rows, glob), 0)
    hit = jnp.where(row == pos_ref[...], 1.0, 0.0).astype(jnp.bfloat16)
    contract = (((0,), (0,)), ((), ()))
    for i, x_ref in enumerate(x_refs):
        for out_ref, which in ((own_ref, core), (sib_ref, 1 - core)):
            x = x_ref[:, pl.ds(pl.multiple_of(which * half, half), half)]
            picked = lax.dot_general(hit, x, contract, preferred_element_type=jnp.float32)
            out_ref[i * glob : (i + 1) * glob, :] = picked.astype(jnp.bfloat16)
            if len(x_refs) > 1:
                edge = pl.multiple_of(core * (rows - BLK), BLK)
                out_ref[(2 + i) * glob : (2 + i) * glob + BLK, :] = x_ref[
                    pl.ds(edge, BLK), pl.ds(pl.multiple_of(which * half, half), half)
                ]


def prepare_kernel(q_own_ref, q_sib_ref, k_own_ref, k_sib_ref, v_own_ref, v_sib_ref, q_t_ref, k_ref, v_t_ref, v_all):
    rows = q_own_ref.shape[0]
    half = k_ref.shape[1]
    core, _ = device_place()
    cols = pl.ds(pl.multiple_of(core * half, half), half)
    zero = jnp.zeros((BLK, half), jnp.bfloat16)
    for ref in (k_ref, v_all):
        ref[:BLK, :] = zero
        ref[BLK + CORES * rows :, :] = zero
    for which, k_from, v_from in ((core, k_own_ref, v_own_ref), (1 - core, k_sib_ref, v_sib_ref)):
        at = pl.ds(pl.multiple_of(which * rows + BLK, BLK), rows)
        k_ref[at, :] = k_from[:, cols]
        v_all[at, :] = v_from[:, cols]

    def turn(head, carry):
        lanes = pl.ds(pl.multiple_of(head * LANES, LANES), LANES)
        source = pl.ds(pl.multiple_of(core * half + head * LANES, LANES), LANES)
        v_t_ref[lanes, :] = jnp.transpose(v_all[:, lanes])
        q_t_ref[lanes, pl.ds(pl.multiple_of(core * rows, LANES), rows)] = jnp.transpose(q_own_ref[:, source])
        q_t_ref[lanes, pl.ds(pl.multiple_of((1 - core) * rows, LANES), rows)] = jnp.transpose(q_sib_ref[:, source])
        return carry

    lax.fori_loop(0, half // LANES, turn, 0)


def global_kernel(scale2, q_a_ref, q_b_ref, k_ref, v_t_ref, out_ref, s_buf, e_buf):
    glob, half = q_a_ref.shape
    head_size = LANES
    pairs = half // (2 * head_size)
    tokens = k_ref.shape[0] - 2 * BLK
    row = lax.broadcasted_iota(jnp.int32, (2 * glob, 2 * head_size), 0)
    col = lax.broadcasted_iota(jnp.int32, (2 * glob, 2 * head_size), 1)
    keep = (row < glob) == (col < head_size)
    lane = lax.broadcasted_iota(jnp.int32, (head_size, LANES), 1)
    for pair in range(pairs):
        cols = slice(2 * pair * head_size, 2 * (pair + 1) * head_size)
        q = q_a_ref[:, cols] + q_b_ref[:, cols]
        doubled = jnp.concatenate([q, q], axis=0)
        diag = jnp.where(keep, doubled, jnp.zeros_like(doubled))
        s_buf[pair] = dot_t(k_ref[BLK : BLK + tokens, cols], diag)
    stats = []
    for pair in range(pairs):
        s = s_buf[pair]
        peak = jnp.max(s, axis=0, keepdims=True)
        e = jnp.exp2((s - peak) * scale2)
        stats.append((peak, jnp.sum(e, axis=0, keepdims=True)))
        zero = jnp.zeros((BLK, LANES), jnp.bfloat16)
        e_buf[pair, :BLK] = zero
        e_buf[pair, BLK + tokens :] = zero
        e_buf[pair, BLK : BLK + tokens] = e.astype(jnp.bfloat16)
    for pair in range(pairs):
        rows = slice(2 * pair * head_size, 2 * (pair + 1) * head_size)
        acc = dot_n(v_t_ref[rows, :], e_buf[pair])
        peak, total = stats[pair]
        out = jnp.where(lane < glob, acc[:head_size], acc[head_size:]) / total
        put_message(out_ref, pair, out, peak, total)


def merge_kernel(scale2, a_ref, b_ref, out_ref):
    head_size = a_ref.shape[1] - STAT_ROWS
    for pair in range(a_ref.shape[0]):
        a = get_message(a_ref, pair, head_size)
        b = get_message(b_ref, pair, head_size)
        put_message(out_ref, pair, *merged(a, b, scale2))


def final_kernel(scale2, a_ref, b_ref, w_ref, pos_ref, win_ref, own_ref, sib_ref):
    pairs = a_ref.shape[0]
    head_size = a_ref.shape[1] - STAT_ROWS
    glob = pos_ref.shape[0]
    core, chip = device_place()
    lane = lax.broadcasted_iota(jnp.int32, (head_size, LANES), 1)
    lin = jnp.zeros((1, LANES), jnp.float32)
    sq = jnp.zeros((1, LANES), jnp.float32)
    for pair in range(pairs):
        a = get_message(a_ref, pair, head_size)
        b = get_message(b_ref, pair, head_size)
        out, _, _ = merged(a, b, scale2)
        w = jnp.where(lane < glob, w_ref[:, 2 * pair : 2 * pair + 1], w_ref[:, 2 * pair + 1 : 2 * pair + 2])
        lin = lin + jnp.sum(out * w, axis=0, keepdims=True)
        sq = sq + jnp.sum(out * out, axis=0, keepdims=True)
    lin = lin + pltpu.roll(lin, glob, 1)
    sq = sq + pltpu.roll(sq, glob, 1)
    parts = [p.astype(jnp.float32) for p in (*pieces(lin), *pieces(sq))] + [jnp.ones((1, LANES), jnp.float32)]
    row = lax.broadcasted_iota(jnp.int32, (16, LANES), 0)
    table = jnp.zeros((16, LANES), jnp.float32)
    for i, part in enumerate(parts):
        table = jnp.where(row == i, jnp.broadcast_to(part, table.shape), table)
    table = table.astype(jnp.bfloat16)[:, :glob]
    pos = pos_ref[...]
    n_pairs = win_ref.shape[1]
    each = n_pairs // CORES
    for out_ref, which in ((own_ref, core), (sib_ref, 1 - core)):
        for j in range(each):
            pair = which * each + j
            token = (chip * n_pairs + pair) * LANES + lax.broadcasted_iota(jnp.int32, (glob, LANES), 1)
            hit = jnp.where(pos == token, 1.0, 0.0).astype(jnp.bfloat16)
            placed = dot_n(table, hit)
            is_glob = placed[6:7] > 0.5
            for i in (0, 1):
                value = placed[3 * i : 3 * i + 1] + placed[3 * i + 1 : 3 * i + 2] + placed[3 * i + 2 : 3 * i + 3]
                out_ref[i, j : j + 1, :] = jnp.where(is_glob, value, win_ref[i, pl.ds(pair, 1), :])


def window_kernel(
    scale2,
    q_t_ref,
    k_ref,
    v_t_ref,
    edge_a_ref,
    edge_b_ref,
    kv_a_ref,
    kv_b_ref,
    w_ref,
    pos_ref,
    out_ref,
    s_buf,
    e_buf,
    bias,
    edges,
    v_glob_t,
):
    half, tokens = q_t_ref.shape
    glob = pos_ref.shape[0]
    n_pairs = tokens // LANES
    core, chip = device_place()
    chips = lax.axis_size("seq") // CORES
    lane = lax.broadcasted_iota(jnp.int32, (BLK, LANES), 1)
    left = lane < BLK
    wide_left = lax.broadcasted_iota(jnp.int32, (LANES, LANES), 1) < BLK
    glob_block = pos_ref[...] // BLK
    for j in range(n_pairs):
        block = (chip * n_pairs + j) * (LANES // BLK) + lax.broadcasted_iota(jnp.int32, (glob, LANES), 1) // BLK
        bias[j] = jnp.where(jnp.abs(glob_block - block) > 1, 0.0, NEG)
    first_bias = jnp.where(left & (chip == 0), NEG, 0.0)
    last_bias = jnp.where((~left) & (chip == chips - 1), NEG, 0.0)

    @pl.when(core == 1)
    def _():
        edges[0] = edge_a_ref[...]
        edges[1] = edge_b_ref[...]

    @pl.when(core == 0)
    def _():
        edges[0] = edge_b_ref[...]
        edges[1] = edge_a_ref[...]

    def one_head(head, carry):
        cols = pl.ds(pl.multiple_of(head * LANES, LANES), LANES)
        kg = kv_a_ref[:glob, cols] + kv_b_ref[:glob, cols]
        for j in range(n_pairs):
            q = q_t_ref[cols, j * LANES : (j + 1) * LANES]
            if j == 0:
                k = jnp.concatenate([edges[0, :BLK, cols], k_ref[BLK : 4 * BLK, cols]], axis=0)
            elif j == n_pairs - 1:
                k = jnp.concatenate([k_ref[j * LANES : j * LANES + 3 * BLK, cols], edges[1, :BLK, cols]], axis=0)
            else:
                k = k_ref[j * LANES : (j + 2) * LANES, cols]
            s_buf[j, : 4 * BLK] = dot_n(k, q)
            s_buf[j, 4 * BLK :] = dot_n(kg, q)
        inverses = []
        for j in range(n_pairs):
            far = s_buf[j, 4 * BLK :] + bias[j]
            ends = jnp.where(left, s_buf[j, :BLK], s_buf[j, 3 * BLK : 4 * BLK])
            if j == 0:
                ends = ends + first_bias
            if j == n_pairs - 1:
                ends = ends + last_bias
            mid = s_buf[j, BLK : 3 * BLK]
            peak = jnp.maximum(jnp.maximum(ends, far), jnp.maximum(mid[:BLK], mid[BLK:]))
            peak = jnp.max(peak, axis=0, keepdims=True)
            e_ends = jnp.exp2((ends - peak) * scale2)
            e_mid = jnp.exp2((mid - peak) * scale2)
            e_far = jnp.exp2((far - peak) * scale2)
            total = jnp.sum(e_ends + e_far + e_mid[:BLK] + e_mid[BLK:], axis=0, keepdims=True)
            zero = jnp.zeros_like(e_ends)
            e_buf[j, :BLK] = jnp.where(left, e_ends, zero).astype(jnp.bfloat16)
            e_buf[j, BLK : 3 * BLK] = e_mid.astype(jnp.bfloat16)
            e_buf[j, 3 * BLK : 4 * BLK] = jnp.where(left, zero, e_ends).astype(jnp.bfloat16)
            e_buf[j, 4 * BLK :] = e_far.astype(jnp.bfloat16)
            inverses.append(1.0 / total)
        vg = kv_a_ref[glob:, cols] + kv_b_ref[glob:, cols]
        vg_t = jnp.transpose(vg)
        turned = jnp.transpose(jnp.concatenate([edges[0, BLK:, cols], edges[1, BLK:, cols]], axis=0))
        w = jnp.broadcast_to(w_ref[head], (LANES, LANES))
        lins, sqs = [], []
        for j in range(n_pairs):
            v_0 = v_t_ref[cols, j * LANES : (j + 1) * LANES]
            v_1 = v_t_ref[cols, (j + 1) * LANES : (j + 2) * LANES]
            if j == 0:
                v_0 = jnp.where(wide_left, turned, v_0)
            if j == n_pairs - 1:
                v_1 = jnp.where(wide_left, v_1, turned)
            acc = dot_n(jnp.concatenate([v_0, v_1], axis=1), e_buf[j, : 4 * BLK]) + dot_n(vg_t, e_buf[j, 4 * BLK :])
            lins.append(jnp.sum(acc * w, axis=0, keepdims=True) * inverses[j])
            sqs.append(jnp.sum(acc * acc, axis=0, keepdims=True) * (inverses[j] * inverses[j]))
        lin, sq = carry
        return lin + jnp.concatenate(lins, axis=0), sq + jnp.concatenate(sqs, axis=0)

    none = jnp.zeros((n_pairs, LANES), jnp.float32)
    lin, sq = lax.fori_loop(0, half // LANES, one_head, (none, none))
    out_ref[0] = lin
    out_ref[1] = sq


def call(kernel, name, outs, args, scratch=()):
    spec = pl.BlockSpec(memory_space=pltpu.VMEM)
    single = not isinstance(outs, list)
    shapes = [outs] if single else outs
    result = pl.pallas_call(
        kernel,
        in_specs=[spec] * len(args),
        out_specs=[spec] * len(shapes),
        out_shape=[pltpu.VMEM(shape, dtype) for shape, dtype in shapes],
        scratch_shapes=[pltpu.VMEM(shape, dtype) for shape, dtype in scratch],
        compiler_params=pltpu.CompilerParams(vmem_limit_bytes=16 * 1024 * 1024),
        name=name,
    )(*[pltpu.with_memory_space_constraint(x, pltpu.VMEM) for x in args])
    return result[0] if single else result


def on_device(queries, keys, values, global_positions, score_weight):
    rows, model_width = queries.shape
    head_size = model_width // HEADS
    half = model_width // CORES
    half_heads = HEADS // CORES
    glob = global_positions.shape[0]
    seq_count = lax.axis_size("seq")
    chips = seq_count // CORES
    core = lax.axis_index("seq") % CORES
    scale2 = head_size ** (-0.5) * LOG2E
    bf16 = jnp.bfloat16
    f32 = jnp.float32
    rounds = int(math.log2(chips))
    tokens = CORES * rows
    n_pairs = tokens // LANES

    def swap(x, mask):
        return lax.ppermute(x, "seq", [(i, i ^ mask) for i in range(seq_count)])

    def shift(x, even, odd):
        moves = [(i, i + (odd if i % CORES else even) * CORES) for i in range(seq_count)]
        return lax.ppermute(x, "seq", [(i, to) for i, to in moves if 0 <= to < seq_count])

    row_positions = global_positions.reshape(1, glob)
    positions = global_positions.reshape(glob, 1)
    small = ((glob, half), bf16)
    big = ((2 * glob + 2 * BLK, half), bf16)
    q_own, q_sib = call(
        functools.partial(select_kernel, None, half), "select_queries", [small, small], [row_positions, queries]
    )
    kv_own, kv_sib = call(
        functools.partial(select_kernel, None, half), "select_keys_values", [big, big], [row_positions, keys, values]
    )
    q_near = q_own + swap(q_sib, 1)
    kv_recv = swap(kv_sib, 1)
    for r in range(1, rounds):
        q_near = q_near + swap(q_near, 1 << r)
    q_far = swap(q_near, 1 << rounds)

    k_other, v_other, q_other = swap(keys, 1), swap(values, 1), swap(queries, 1)
    kv_near = kv_own[: 2 * glob] + kv_recv[: 2 * glob]
    edge_a = shift(kv_own[2 * glob :], -1, 1)
    edge_b = shift(kv_recv[2 * glob :], 1, -1)
    for r in range(1, rounds):
        kv_near = kv_near + swap(kv_near, 1 << r)
    kv_far = swap(kv_near, 1 << rounds)

    q_t, k_all, v_t = call(
        prepare_kernel,
        "prepare",
        [((half, tokens), bf16), ((tokens + 2 * BLK, half), bf16), ((half, tokens + 2 * BLK), bf16)],
        [queries, q_other, keys, k_other, values, v_other],
        [((tokens + 2 * BLK, half), bf16)],
    )
    part = ((half_heads // 2, head_size + STAT_ROWS, LANES), bf16)
    message = call(
        functools.partial(global_kernel, scale2),
        "global_partial",
        part,
        [q_near, q_far, k_all, v_t],
        [((half_heads // 2, tokens, LANES), f32), ((half_heads // 2, tokens + 2 * BLK, LANES), bf16)],
    )
    for r in range(1, rounds):
        message = call(
            functools.partial(merge_kernel, scale2), "merge_partial", part, [message, swap(message, 1 << r)]
        )
    message_far = swap(message, 1 << rounds)

    weight_rows = lax.dynamic_slice_in_dim(score_weight.reshape(HEADS, head_size), core * half_heads, half_heads, 0)
    window = call(
        functools.partial(window_kernel, scale2),
        "window_attention",
        ((2, n_pairs, LANES), f32),
        [q_t, k_all, v_t, edge_a, edge_b, kv_near, kv_far, weight_rows.reshape(half_heads, head_size, 1), positions],
        [
            ((n_pairs, 4 * BLK + glob, LANES), f32),
            ((n_pairs, 4 * BLK + glob, LANES), bf16),
            ((n_pairs, glob, LANES), f32),
            ((2, 2 * BLK, half), bf16),
            ((LANES, glob), bf16),
        ],
    )
    share = ((2, n_pairs // CORES, LANES), f32)
    mine, theirs = call(
        functools.partial(final_kernel, scale2),
        "place_global",
        [share, share],
        [message, message_far, jnp.transpose(weight_rows), positions, window],
    )
    theirs = swap(theirs, 1)
    lin = mine[0] + theirs[0]
    sq = mine[1] + theirs[1]
    return (lin * lax.rsqrt(sq * (1.0 / model_width) + 1e-06)).reshape(rows)


def solution(mesh):
    placed = (
        P(("doc", "seq"), None),
        P(("doc", "seq"), None),
        P(("doc", "seq"), None),
        P("doc"),
        P(),
    )
    return jax.shard_map(
        on_device, mesh=mesh, in_specs=placed, out_specs=P(("doc", "seq")), check_vma=False
    )
```

time: 75.6 us -> 66.1 us (0.87)
  Pallas kernels: 21.1 us -> 10.9 us
  waiting for transfers between devices: 15.3 us -> 25.5 us
  starting transfers between devices: 12.4 us -> 19.7 us
  local copies, waits for them, and re-layouts: 15.2 us -> 7.98 us
  other arithmetic: 8.21 us -> 1.58 us
  matrix products: 2.72 us -> 0 us
    pallas_call x4 -> x7, Pallas kernels: 21.1 us -> 10.9 us  [call(): pl.pallas_call(kernel, in_specs=[spec] * len(args), out_specs=[spec] * le...]
    ppermute x10 -> x12, waiting for transfers between devices: 14.9 us -> 22.7 us  [swap(): return lax.ppermute(x, 'seq', [(i, i ^ mask) for i in range(seq_count)])]
    ppermute x10 -> x12, starting transfers between devices: 8.8 us -> 13.9 us  [swap(): return lax.ppermute(x, 'seq', [(i, i ^ mask) for i in range(seq_count)])]
    dynamic_slice x4 -> x0, local copies, waits for them, and re-layouts: 4.62 us -> none  [columns(): return lax.dynamic_slice_in_dim(x, which * half, half, axis=1)]
    add x7 -> x4, other arithmetic: 4.57 us -> 0.99 us  [the longest x1 0.85 us: on_device(): kv_near = kv_own[:2 * glob] + kv_recv[:2 * glob]]
    concatenate x4 -> x0, other arithmetic: 2.77 us -> none  [the longest x1 1.3 us: on_device(): jnp.concatenate([columns(keys, 1 - core), columns(values, 1 - core)], axi...]
    dot_general x3 -> x0, matrix products: 2.72 us -> none  [on_device(): jnp.dot(select, x, preferred_element_type=f32).astype(bf16)]
    ppermute x2, starting transfers between devices: 3.55 us -> 5.84 us  [shift(): lax.ppermute(x, 'seq', [(i, to) for i, to in moves if 0 <= to < seq_count])]
  transfers between devices with their start and end apart: 12 -> 14, of which waited for: 6 -> 7; matrix products, arithmetic and copies ran while one was open for 19% -> 3% of each run, Pallas kernels for 25% -> 16%
where the time goes in v2:
time: 66.1 us; the launch traced here: 65.8 us
  waiting for transfers between devices  25.5 us (39%)
  starting transfers between devices  19.7 us (30%)
  Pallas kernels  10.9 us (16%)
  local copies, waits for them, and re-layouts  7.98 us (12%)
  other arithmetic  1.58 us (2%)
    ppermute x12, waiting for transfers between devices, swap(): return lax.ppermute(x, 'seq', [(i, i ^ mask) for i in range(seq_count)])  22.7 us
    ppermute x12, starting transfers between devices, swap(): return lax.ppermute(x, 'seq', [(i, i ^ mask) for i in range(seq_count)])  13.9 us
    pallas_call x7, Pallas kernels, call(): pl.pallas_call(kernel, in_specs=[spec] * len(args), out_specs=[spec] * le...  10.9 us
    unnamed x25, local copies, waits for them, and re-layouts  7.05 us
    ppermute x2, starting transfers between devices, shift(): lax.ppermute(x, 'seq', [(i, to) for i, to in moves if 0 <= to < seq_count])  5.84 us
    ppermute x2, waiting for transfers between devices, shift(): lax.ppermute(x, 'seq', [(i, to) for i, to in moves if 0 <= to < seq_count])  2.75 us
  transfers between devices with their start and end apart: 14, of which 7 were waited for; matrix products, arithmetic and copies ran while one was open for 3% of the time, Pallas kernels for 16%

profile of v2, /device:TPU:0, one launch (start us, length us, event | category | flops | bytes accessed | tf_op | source)
XLA Modules:
  0.0 65.8 jit_solution(5742583860281067420)
XLA Ops:
  0.0 0.5 collective-permute-start.3
  0.5 0.1 collective-permute-start.4
  0.5 0.4 collective-permute-start.5
  1.0 1.4 %copy-done.4 = bf16[384,2048]{1,0:T(8,128)(2,1)S(1)} copy-done((bf16[384,2048]{1,0:T(8,128)(2,1)S(1)}, bf16[384,2048]{1,0:T(8,128)(2,1)}, u32[]{:S(2)}) %copy-start.4) | copy-done | bytes 1572888
  2.4 1.4 %copy-done.6 = bf16[384,2048]{1,0:T(8,128)(2,1)S(1)} copy-done((bf16[384,2048]{1,0:T(8,128)(2,1)S(1)}, bf16[384,2048]{1,0:T(8,128)(2,1)}, u32[]{:S(2)}) %copy-start.6) | copy-done | bytes 1572888
  3.8 0.7 copy-done.10
  4.4 0.7 %select_keys_values.1 = (bf16[256,1024]{1,0:T(8,128)(2,1)S(1)}, bf16[256,1024]{1,0:T(8,128)(2,1)S(1)}) custom-call(s32[1,64]{1,0:T(1,128)S(1)} %bitcast.10, bf16[384,2048]{1,0:T(8,128)(2,1)S(1)} %copy-done.4, bf16[384,2048]{1,0:T(8,128)(2,1)S(1)} %copy-done.6), custom_call_target="tpu_custom_call" | custom-call | tf_op jit(solution)/shard_map/select_keys_values/pallas_call | solution.py:302
  5.2 0.1 collective-permute-start.9
  5.3 0.5 copy-done.3
  5.9 0.4 select_queries.1
  6.3 0.0 copy-start.5
  6.3 0.1 collective-permute-start
  6.4 2.5 %collective-permute-done = bf16[64,1024]{1,0:T(8,128)(2,1)S(1)} collective-permute-done((bf16[64,1024]{1,0:T(8,128)(2,1)S(1)}, bf16[64,1024]{1,0:T(8,128)(2,1)S(1)}, u32[]{:S(2)}, u32[]{:S(2)}) %collective-permute-start) | collective-permute-done | bytes 131104 | tf_op jit(solution)/shard_map/ppermute | solution.py:331
  9.0 3.0 %collective-permute-start.1 = (bf16[64,1024]{1,0:T(8,128)(2,1)S(1)}, bf16[64,1024]{1,0:T(8,128)(2,1)S(1)}, u32[]{:S(2)}, u32[]{:S(2)}) collective-permute-start(bf16[64,1024]{1,0:T(8,128)(2,1)S(1)} %add.39), channel_id=1, source_target_pairs={{0,2},{1,3},{2,0},{3,1},{4,6},{5,7},{6,4},{7,5},{8,10},{9,11},{10,... | collective-permute-start | bytes 393224 | tf_op jit(solution)/shard_map/ppermute | solution.py:331
  12.0 0.0 collective-permute-done.9
  12.0 0.8 %slice_add_fusion = (bf16[128,1024]{1,0:T(8,128)(2,1)S(1)}, bf16[128,1024]{1,0:T(8,128)(2,1)}, bf16[128,1024]{1,0:T(8,128)(2,1)}) fusion(bf16[256,1024]{1,0:T(8,128)(2,1)S(1)} %collective-permute-done.9, bf16[256,1024]{1,0:T(8,128)(2,1)S(1)} %get-tuple-element.19), kind=kLoop, calls=%fused_computation | loop fusion | flops 131072 | bytes 1835008 | tf_op jit(solution)/shard_map/add | solution.py:354
  12.8 0.0 collective-permute-start.11
  12.9 3.4 %collective-permute-done.1 = bf16[64,1024]{1,0:T(8,128)(2,1)S(1)} collective-permute-done((bf16[64,1024]{1,0:T(8,128)(2,1)S(1)}, bf16[64,1024]{1,0:T(8,128)(2,1)S(1)}, u32[]{:S(2)}, u32[]{:S(2)}) %collective-permute-start.1) | collective-permute-done | bytes 131104 | tf_op jit(solution)/shard_map/ppermute | solution.py:331
  16.3 2.9 %collective-permute-start.2 = (bf16[64,1024]{1,0:T(8,128)(2,1)S(1)}, bf16[64,1024]{1,0:T(8,128)(2,1)S(1)}, u32[]{:S(2)}, u32[]{:S(2)}) collective-permute-start(bf16[64,1024]{1,0:T(8,128)(2,1)S(1)} %add.40.q_a_ref), channel_id=1, source_target_pairs={{0,4},{1,5},{2,6},{3,7},{4,0},{5,1},{6,2},{7,3},{8,12},{9,13},{10,... | collective-permute-start | bytes 393224 | tf_op jit(solution)/shard_map/ppermute | solution.py:331
  19.2 0.0 collective-permute-done.3.q_sib_ref
  19.3 0.0 collective-permute-done.4.k_sib_ref
  19.3 0.0 collective-permute-done.5.v_sib_ref
  19.3 1.6 %prepare.1 = (bf16[1024,768]{1,0:T(8,128)(2,1)S(1)}, bf16[896,1024]{1,0:T(8,128)(2,1)S(1)}, bf16[1024,896]{1,0:T(8,128)(2,1)S(1)}) custom-call(bf16[384,2048]{1,0:T(8,128)(2,1)S(1)} %copy-done.3, bf16[384,2048]{1,0:T(8,128)(2,1)S(1)} %collective-permute-done.3.q_sib_ref, bf16[384,2048]{1,0:T(8,128)(2,1)S(1)} %copy-done.5, ...), custom_call_target="tpu_custom_call" | custom-call | tf_op jit(solution)/shard_map/prepare/pallas_call | solution.py:302
  21.0 2.6 %collective-permute-done.2.q_b_ref = bf16[64,1024]{1,0:T(8,128)(2,1)S(1)} collective-permute-done((bf16[64,1024]{1,0:T(8,128)(2,1)S(1)}, bf16[64,1024]{1,0:T(8,128)(2,1)S(1)}, u32[]{:S(2)}, u32[]{:S(2)}) %collective-permute-start.2) | collective-permute-done | bytes 131104 | tf_op jit(solution)/shard_map/ppermute | solution.py:331
  23.5 1.4 %global_partial.1.a_ref = bf16[4,144,128]{2,1,0:T(8,128)(2,1)S(1)} custom-call(bf16[64,1024]{1,0:T(8,128)(2,1)S(1)} %add.40.q_a_ref, bf16[64,1024]{1,0:T(8,128)(2,1)S(1)} %collective-permute-done.2.q_b_ref, bf16[896,1024]{1,0:T(8,128)(2,1)S(1)} %get-tuple-element.16.k_ref, bf16[1024,896]{1,0:T(8,128)(2,1)S(1)} %get-tuple-element.17.v_t_ref), custom_call_target="tpu_custom_call" | custom-call | tf_op jit(solution)/shard_map/global_partial/pallas_call | solution.py:302
  24.9 3.5 %collective-permute-start.6 = (bf16[4,144,128]{2,1,0:T(8,128)(2,1)S(1)}, bf16[4,144,128]{2,1,0:T(8,128)(2,1)S(1)}, u32[]{:S(2)}, u32[]{:S(2)}) collective-permute-start(bf16[4,144,128]{2,1,0:T(8,128)(2,1)S(1)} %global_partial.1.a_ref), channel_id=1, source_target_pairs={{0,2},{1,3},{2,0},{3,1},{4,6},{5,7},{6,4},{7,5},{8,10},{9,11},{10,... | collective-permute-start | bytes 442376 | tf_op jit(solution)/shard_map/ppermute | solution.py:331
  28.4 1.3 %collective-permute-start.8 = (bf16[128,1024]{1,0:T(8,128)(2,1)}, bf16[128,1024]{1,0:T(8,128)(2,1)S(1)}, u32[]{:S(2)}, u32[]{:S(2)}) collective-permute-start(bf16[128,1024]{1,0:T(8,128)(2,1)} %get-tuple-element.24), channel_id=1, source_target_pairs={{1,3},{2,0},{3,5},{4,2},{5,7},{6,4},{9,11},{10,8},{11,13},{12,10},... | collective-permute-start | bytes 786440 | tf_op jit(solution)/shard_map/ppermute | solution.py:335
  29.7 4.6 %collective-permute-start.10 = (bf16[128,1024]{1,0:T(8,128)(2,1)}, bf16[128,1024]{1,0:T(8,128)(2,1)S(1)}, u32[]{:S(2)}, u32[]{:S(2)}) collective-permute-start(bf16[128,1024]{1,0:T(8,128)(2,1)} %get-tuple-element.25), channel_id=1, source_target_pairs={{0,2},{2,4},{3,1},{4,6},{5,3},{7,5},{8,10},{10,12},{11,9},{12,14},... | collective-permute-start | bytes 786440 | tf_op jit(solution)/shard_map/ppermute | solution.py:335
  34.3 0.0 collective-permute-done.11
  34.3 0.1 add.44.kv_a_ref
  34.4 2.4 %collective-permute-start.12 = (bf16[128,1024]{1,0:T(8,128)(2,1)S(1)}, bf16[128,1024]{1,0:T(8,128)(2,1)}, u32[]{:S(2)}, u32[]{:S(2)}) collective-permute-start(bf16[128,1024]{1,0:T(8,128)(2,1)S(1)} %add.44.kv_a_ref), channel_id=1, source_target_pairs={{0,4},{1,5},{2,6},{3,7},{4,0},{5,1},{6,2},{7,3},{8,12},{9,13},{10,... | collective-permute-start | bytes 786440 | tf_op jit(solution)/shard_map/ppermute | solution.py:331
  36.8 0.0 collective-permute-done.6.b_ref
  36.8 0.1 merge_partial.1.a_ref
  36.9 0.7 collective-permute-start.7
  37.5 0.1 copy.15
  37.6 0.1 copy.12.pos_ref
  37.7 0.8 %copy.10.w_ref = f32[8,128,1]{2,1,0:T(8,128)S(1)} copy(f32[8,128,1]{0,1,2:T(8,128)S(1)} %bitcast.8) | data formatting | bytes 8192 | tf_op jit(solution)/shard_map/reshape | solution.py:387
  38.6 1.1 %collective-permute-done.8.edge_a_ref = bf16[128,1024]{1,0:T(8,128)(2,1)S(1)} collective-permute-done((bf16[128,1024]{1,0:T(8,128)(2,1)}, bf16[128,1024]{1,0:T(8,128)(2,1)S(1)}, u32[]{:S(2)}, u32[]{:S(2)}) %collective-permute-start.8) | collective-permute-done | bytes 262176 | tf_op jit(solution)/shard_map/ppermute | solution.py:335
  39.7 1.7 %collective-permute-done.10.edge_b_ref = bf16[128,1024]{1,0:T(8,128)(2,1)S(1)} collective-permute-done((bf16[128,1024]{1,0:T(8,128)(2,1)}, bf16[128,1024]{1,0:T(8,128)(2,1)S(1)}, u32[]{:S(2)}, u32[]{:S(2)}) %collective-permute-start.10) | collective-permute-done | bytes 262176 | tf_op jit(solution)/shard_map/ppermute | solution.py:335
  41.3 13.1 %collective-permute-done.12.kv_b_ref = bf16[128,1024]{1,0:T(8,128)(2,1)} collective-permute-done((bf16[128,1024]{1,0:T(8,128)(2,1)S(1)}, bf16[128,1024]{1,0:T(8,128)(2,1)}, u32[]{:S(2)}, u32[]{:S(2)}) %collective-permute-start.12) | collective-permute-done | bytes 262176 | tf_op jit(solution)/shard_map/ppermute | solution.py:331
  54.4 1.5 %copy-done.2 = bf16[1024,896]{1,0:T(8,128)(2,1)S(1)} copy-done((bf16[1024,896]{1,0:T(8,128)(2,1)S(1)}, bf16[1024,896]{1,0:T(8,128)(2,1)}, u32[]{:S(2)}) %copy-start.2) | copy-done | bytes 1835032
  55.9 1.4 %copy-done.9 = bf16[1024,768]{1,0:T(8,128)(2,1)S(1)} copy-done((bf16[1024,768]{1,0:T(8,128)(2,1)S(1)}, bf16[1024,768]{1,0:T(8,128)(2,1)}, u32[]{:S(2)}) %copy-start.9) | copy-done | bytes 1572888
  57.3 6.1 %window_attention.1.win_ref = f32[2,6,128]{2,1,0:T(8,128)S(1)} custom-call(bf16[1024,768]{1,0:T(8,128)(2,1)S(1)} %copy-done.9, bf16[896,1024]{1,0:T(8,128)(2,1)S(1)} %get-tuple-element.16.k_ref, bf16[1024,896]{1,0:T(8,128)(2,1)S(1)} %copy-done.2, bf16[128,1024]{1,0:T(8,128)(2,1)S(1)} %collective-permute-done.8.edge_a_ref, ...), custom_call_target="tpu_custom_call" | custom-call | tf_op jit(solution)/shard_map/window_attention/pallas_call | solution.py:302
  63.5 0.0 collective-permute-done.7.b_ref
  63.5 0.5 place_global.1
  64.0 0.1 collective-permute-start.13
  64.1 1.2 %collective-permute-done.13 = f32[2,3,128]{2,1,0:T(4,128)S(1)} collective-permute-done((f32[2,3,128]{2,1,0:T(4,128)S(1)}, f32[2,3,128]{2,1,0:T(4,128)S(1)}, u32[]{:S(2)}, u32[]{:S(2)}) %collective-permute-start.13) | collective-permute-done | bytes 3104 | tf_op jit(solution)/shard_map/ppermute | solution.py:331
  65.2 0.6 fusion.4
  (20 shorter events, 0.1 us)
Async XLA Ops:
  0.0 37.5 %copy-start = (f32[2048]{0:T(1024)S(1)}, f32[2048]{0:T(1024)}, u32[]{:S(2)}) copy-start(f32[2048]{0:T(1024)} %param.9) | copy-start | bytes 24580
  0.0 19.2 %collective-permute-start.3 = (bf16[384,2048]{1,0:T(8,128)(2,1)}, bf16[384,2048]{1,0:T(8,128)(2,1)S(1)}, u32[]{:S(2)}, u32[]{:S(2)}) collective-permute-start(bf16[384,2048]{1,0:T(8,128)(2,1)} %q_own_ref.1), channel_id=1, source_target_pairs={{0,1},{1,0},{2,3},{3,2},{4,5},{5,4},{6,7},{7,6},{8,9},{9,8},{10,11... | collective-permute-start | bytes 4718600 | tf_op jit(solution)/shard_map/ppermute | solution.py:331
  0.5 18.8 %collective-permute-start.4 = (bf16[384,2048]{1,0:T(8,128)(2,1)}, bf16[384,2048]{1,0:T(8,128)(2,1)S(1)}, u32[]{:S(2)}, u32[]{:S(2)}) collective-permute-start(bf16[384,2048]{1,0:T(8,128)(2,1)} %refs_0_.3), channel_id=1, source_target_pairs={{0,1},{1,0},{2,3},{3,2},{4,5},{5,4},{6,7},{7,6},{8,9},{9,8},{10,11... | collective-permute-start | bytes 4718600 | tf_op jit(solution)/shard_map/ppermute | solution.py:331
  0.5 18.7 %collective-permute-start.5 = (bf16[384,2048]{1,0:T(8,128)(2,1)}, bf16[384,2048]{1,0:T(8,128)(2,1)S(1)}, u32[]{:S(2)}, u32[]{:S(2)}) collective-permute-start(bf16[384,2048]{1,0:T(8,128)(2,1)} %refs_1_.1), channel_id=1, source_target_pairs={{0,1},{1,0},{2,3},{3,2},{4,5},{5,4},{6,7},{7,6},{8,9},{9,8},{10,11... | collective-permute-start | bytes 4718600 | tf_op jit(solution)/shard_map/ppermute | solution.py:331
  1.0 1.4 %copy-start.4 = (bf16[384,2048]{1,0:T(8,128)(2,1)S(1)}, bf16[384,2048]{1,0:T(8,128)(2,1)}, u32[]{:S(2)}) copy-start(bf16[384,2048]{1,0:T(8,128)(2,1)} %refs_0_.3) | copy-start | bytes 4718596
  2.4 1.4 %copy-start.6 = (bf16[384,2048]{1,0:T(8,128)(2,1)S(1)}, bf16[384,2048]{1,0:T(8,128)(2,1)}, u32[]{:S(2)}) copy-start(bf16[384,2048]{1,0:T(8,128)(2,1)} %refs_1_.1) | copy-start | bytes 4718596
  3.8 0.7 copy-start.10
  4.4 1.4 %copy-start.3 = (bf16[384,2048]{1,0:T(8,128)(2,1)S(1)}, bf16[384,2048]{1,0:T(8,128)(2,1)}, u32[]{:S(2)}) copy-start(bf16[384,2048]{1,0:T(8,128)(2,1)} %q_own_ref.1) | copy-start | bytes 4718596
  5.2 6.8 %collective-permute-start.9 = (bf16[256,1024]{1,0:T(8,128)(2,1)S(1)}, bf16[256,1024]{1,0:T(8,128)(2,1)S(1)}, u32[]{:S(2)}, u32[]{:S(2)}) collective-permute-start(bf16[256,1024]{1,0:T(8,128)(2,1)S(1)} %get-tuple-element.20), channel_id=1, source_target_pairs={{0,1},{1,0},{2,3},{3,2},{4,5},{5,4},{6,7},{7,6},{8,9},{9,8},{10,11... | collective-permute-start | bytes 1572872 | tf_op jit(solution)/shard_map/ppermute | solution.py:331
  5.8 13.4 %copy-start.7 = (bf16[384,2048]{1,0:T(8,128)(2,1)S(1)}, bf16[384,2048]{1,0:T(8,128)(2,1)}, u32[]{:S(2)}) copy-start(bf16[384,2048]{1,0:T(8,128)(2,1)} %refs_1_.1) | copy-start | bytes 4718596
  6.3 13.0 %copy-start.5 = (bf16[384,2048]{1,0:T(8,128)(2,1)S(1)}, bf16[384,2048]{1,0:T(8,128)(2,1)}, u32[]{:S(2)}) copy-start(bf16[384,2048]{1,0:T(8,128)(2,1)} %refs_0_.3) | copy-start | bytes 4718596
  6.3 2.6 %collective-permute-start = (bf16[64,1024]{1,0:T(8,128)(2,1)S(1)}, bf16[64,1024]{1,0:T(8,128)(2,1)S(1)}, u32[]{:S(2)}, u32[]{:S(2)}) collective-permute-start(bf16[64,1024]{1,0:T(8,128)(2,1)S(1)} %get-tuple-element.15), channel_id=1, source_target_pairs={{0,1},{1,0},{2,3},{3,2},{4,5},{5,4},{6,7},{7,6},{8,9},{9,8},{10,11... | collective-permute-start | bytes 393224 | tf_op jit(solution)/shard_map/ppermute | solution.py:331
  9.0 7.3 %collective-permute-start.1 = (bf16[64,1024]{1,0:T(8,128)(2,1)S(1)}, bf16[64,1024]{1,0:T(8,128)(2,1)S(1)}, u32[]{:S(2)}, u32[]{:S(2)}) collective-permute-start(bf16[64,1024]{1,0:T(8,128)(2,1)S(1)} %add.39), channel_id=1, source_target_pairs={{0,2},{1,3},{2,0},{3,1},{4,6},{5,7},{6,4},{7,5},{8,10},{9,11},{10,... | collective-permute-start | bytes 393224 | tf_op jit(solution)/shard_map/ppermute | solution.py:331
  12.8 21.4 %collective-permute-start.11 = (bf16[128,1024]{1,0:T(8,128)(2,1)S(1)}, bf16[128,1024]{1,0:T(8,128)(2,1)S(1)}, u32[]{:S(2)}, u32[]{:S(2)}) collective-permute-start(bf16[128,1024]{1,0:T(8,128)(2,1)S(1)} %get-tuple-element.23), channel_id=1, source_target_pairs={{0,2},{1,3},{2,0},{3,1},{4,6},{5,7},{6,4},{7,5},{8,10},{9,11},{10,... | collective-permute-start | bytes 786440 | tf_op jit(solution)/shard_map/ppermute | solution.py:331
  16.3 7.2 %collective-permute-start.2 = (bf16[64,1024]{1,0:T(8,128)(2,1)S(1)}, bf16[64,1024]{1,0:T(8,128)(2,1)S(1)}, u32[]{:S(2)}, u32[]{:S(2)}) collective-permute-start(bf16[64,1024]{1,0:T(8,128)(2,1)S(1)} %add.40.q_a_ref), channel_id=1, source_target_pairs={{0,4},{1,5},{2,6},{3,7},{4,0},{5,1},{6,2},{7,3},{8,12},{9,13},{10,... | collective-permute-start | bytes 393224 | tf_op jit(solution)/shard_map/ppermute | solution.py:331
  20.9 4.0 %copy-start.1 = (bf16[1024,896]{1,0:T(8,128)(2,1)}, bf16[1024,896]{1,0:T(8,128)(2,1)S(1)}, u32[]{:S(2)}) copy-start(bf16[1024,896]{1,0:T(8,128)(2,1)S(1)} %get-tuple-element.17.v_t_ref) | copy-start | bytes 5505028
  20.9 4.0 %copy-start.8 = (bf16[1024,768]{1,0:T(8,128)(2,1)}, bf16[1024,768]{1,0:T(8,128)(2,1)S(1)}, u32[]{:S(2)}) copy-start(bf16[1024,768]{1,0:T(8,128)(2,1)S(1)} %get-tuple-element.18.q_t_ref) | copy-start | bytes 4718596
  23.5 14.1 %copy-start.11 = (s32[64]{0:T(128)S(1)}, s32[64]{0:T(128)}, u32[]{:S(2)}) copy-start(s32[64]{0:T(128)} %param.8) | copy-start | bytes 772
  24.9 11.9 %collective-permute-start.6 = (bf16[4,144,128]{2,1,0:T(8,128)(2,1)S(1)}, bf16[4,144,128]{2,1,0:T(8,128)(2,1)S(1)}, u32[]{:S(2)}, u32[]{:S(2)}) collective-permute-start(bf16[4,144,128]{2,1,0:T(8,128)(2,1)S(1)} %global_partial.1.a_ref), channel_id=1, source_target_pairs={{0,2},{1,3},{2,0},{3,1},{4,6},{5,7},{6,4},{7,5},{8,10},{9,11},{10,... | collective-permute-start | bytes 442376 | tf_op jit(solution)/shard_map/ppermute | solution.py:331
  28.4 11.2 %collective-permute-start.8 = (bf16[128,1024]{1,0:T(8,128)(2,1)}, bf16[128,1024]{1,0:T(8,128)(2,1)S(1)}, u32[]{:S(2)}, u32[]{:S(2)}) collective-permute-start(bf16[128,1024]{1,0:T(8,128)(2,1)} %get-tuple-element.24), channel_id=1, source_target_pairs={{1,3},{2,0},{3,5},{4,2},{5,7},{6,4},{9,11},{10,8},{11,13},{12,10},... | collective-permute-start | bytes 786440 | tf_op jit(solution)/shard_map/ppermute | solution.py:335
  29.7 11.6 %collective-permute-start.10 = (bf16[128,1024]{1,0:T(8,128)(2,1)}, bf16[128,1024]{1,0:T(8,128)(2,1)S(1)}, u32[]{:S(2)}, u32[]{:S(2)}) collective-permute-start(bf16[128,1024]{1,0:T(8,128)(2,1)} %get-tuple-element.25), channel_id=1, source_target_pairs={{0,2},{2,4},{3,1},{4,6},{5,3},{7,5},{8,10},{10,12},{11,9},{12,14},... | collective-permute-start | bytes 786440 | tf_op jit(solution)/shard_map/ppermute | solution.py:335
  34.4 20.1 %collective-permute-start.12 = (bf16[128,1024]{1,0:T(8,128)(2,1)S(1)}, bf16[128,1024]{1,0:T(8,128)(2,1)}, u32[]{:S(2)}, u32[]{:S(2)}) collective-permute-start(bf16[128,1024]{1,0:T(8,128)(2,1)S(1)} %add.44.kv_a_ref), channel_id=1, source_target_pairs={{0,4},{1,5},{2,6},{3,7},{4,0},{5,1},{6,2},{7,3},{8,12},{9,13},{10,... | collective-permute-start | bytes 786440 | tf_op jit(solution)/shard_map/ppermute | solution.py:331
  36.9 26.6 %collective-permute-start.7 = (bf16[4,144,128]{2,1,0:T(8,128)(2,1)S(1)}, bf16[4,144,128]{2,1,0:T(8,128)(2,1)S(1)}, u32[]{:S(2)}, u32[]{:S(2)}) collective-permute-start(bf16[4,144,128]{2,1,0:T(8,128)(2,1)S(1)} %merge_partial.1.a_ref), channel_id=1, source_target_pairs={{0,4},{1,5},{2,6},{3,7},{4,0},{5,1},{6,2},{7,3},{8,12},{9,13},{10,... | collective-permute-start | bytes 442376 | tf_op jit(solution)/shard_map/ppermute | solution.py:331
  54.4 1.5 %copy-start.2 = (bf16[1024,896]{1,0:T(8,128)(2,1)S(1)}, bf16[1024,896]{1,0:T(8,128)(2,1)}, u32[]{:S(2)}) copy-start(bf16[1024,896]{1,0:T(8,128)(2,1)} %copy-done.1) | copy-start | bytes 5505028
  55.9 1.4 %copy-start.9 = (bf16[1024,768]{1,0:T(8,128)(2,1)S(1)}, bf16[1024,768]{1,0:T(8,128)(2,1)}, u32[]{:S(2)}) copy-start(bf16[1024,768]{1,0:T(8,128)(2,1)} %copy-done.8) | copy-start | bytes 4718596
  64.0 1.2 %collective-permute-start.13 = (f32[2,3,128]{2,1,0:T(4,128)S(1)}, f32[2,3,128]{2,1,0:T(4,128)S(1)}, u32[]{:S(2)}, u32[]{:S(2)}) collective-permute-start(f32[2,3,128]{2,1,0:T(4,128)S(1)} %get-tuple-element.22), channel_id=1, source_target_pairs={{0,1},{1,0},{2,3},{3,2},{4,5},{5,4},{6,7},{7,6},{8,9},{9,8},{10,11... | collective-permute-start | bytes 9224 | tf_op jit(solution)/shard_map/ppermute | solution.py:331
